TPU v7x, 32 devices: a whole 2x2x4 slice. The times are simulated.
32 devices in a mesh: mem: 4 (over y, core), ctx: 8 (over z, x).
Axes of the slice: x: 2, y: 2, z: 4, core: 2. Of those that a mesh axis runs over, the one named last changes fastest.
Arguments:
- queries: bfloat16 [8, 512, 32, 128], P('ctx', 'mem'), may hold values from -6 to 6
- keys: bfloat16 [8, 512, 32, 128], P('ctx', 'mem'), may hold values from -6 to 6
- values: bfloat16 [8, 512, 32, 128], P('ctx', 'mem'), may hold values from -6 to 6
- log_decay: bfloat16 [8, 512, 32], P('ctx', 'mem'), may hold values from -1 to 0, as said below
- routes: int32 [8, 512, 2], P('ctx', 'mem'), may hold values from 0 to 3, all different within a row; in each aligned block of 128 rows (0 to 127, 128 to 255, ..., all dimensions but the last counted through in order) at most 72 rows name the same one
- route_weight: float32 [8, 512, 2], P('ctx', 'mem'), may hold values from 0.2 to 1
- gain: float32 [4096], replicated, may hold values from 0.25 to 1.75
Outputs:
- layer_out: bfloat16 [8, 512, 32, 128], P('ctx', 'mem')
Inputs may be any that keep to these rules, and one draw needn't show every extreme that they name: `routes`: A token's two memories differ. Among the tokens of one device (an aligned block of 128 tokens) no memory is named by more than 72 tokens, and in some such block a memory is named by exactly 72. `log_decay`: entries are negative.
All inputs are finite; a program needn't handle non-finite values.
Results may differ from a plain program's by a relative error of at most 0.015.
Values may be sent and summed in bfloat16 or wider, within the bound.
No kernel may reach another device: no remote copies, remote signals or barrier semaphores. Data moves between devices by JAX's collectives and lax.ppermute only.
A program may use at most 128 MiB of HBM per device.

v0:
```python
import math

import jax
import jax.numpy as jnp
from jax import lax
from jax.sharding import PartitionSpec as P


def as_sent(array):

    def short(part):
        return part.astype(jnp.bfloat16) if part.dtype == jnp.float32 else part

    return jax.tree.map(short, array)


def split_parts(matrix):
    high = matrix.astype(jnp.bfloat16)
    low = (matrix - high.astype(jnp.float32)).astype(jnp.bfloat16)
    return (high, low)


def head_norm(rows):
    square_mean = jnp.mean(rows * rows, axis=-1, keepdims=True)
    return rows * lax.rsqrt(square_mean + 1e-06)


def local_terms(keys_in, incoming_values, rates_in):
    running_decay = jnp.cumsum(rates_in.astype(jnp.float32), axis=0)
    total = running_decay[-1]
    retained_mask = jnp.exp(total[None, :] - running_decay)
    upper_scaled_state, lower_scaled_state = split_parts(
        keys_in.astype(jnp.float32) * retained_mask[:, :, None]
    )
    state_increment = jnp.einsum(
        "dyn,dye->yne", upper_scaled_state, incoming_values, preferred_element_type=jnp.float32
    )
    state_increment = state_increment + jnp.einsum(
        "dyn,dye->yne", lower_scaled_state, incoming_values, preferred_element_type=jnp.float32
    )
    return (running_decay, jnp.exp(total), state_increment)


def compose_rows(earlier, later):
    return (earlier[0] * later[0], later[0][..., None] * earlier[1] + later[1])


def incoming_state(decay_total, state_increment):
    heads = state_increment.shape[0]
    hdim = state_increment.shape[1]
    flat_rows = heads * hdim
    pieces = (
        lax.all_to_all(
            state_increment.reshape(1, flat_rows, hdim).astype(jnp.bfloat16),
            "ctx",
            split_axis=1,
            concat_axis=0,
            tiled=True,
        ).astype(jnp.float32),
        lax.all_to_all(
            jnp.repeat(decay_total, hdim).reshape(1, flat_rows).astype(jnp.bfloat16),
            "ctx",
            split_axis=1,
            concat_axis=0,
            tiled=True,
        ).astype(jnp.float32),
    )
    inclusive = lax.associative_scan(compose_rows, (pieces[1], pieces[0]), axis=0)
    shifted = jnp.concatenate([jnp.zeros_like(inclusive[1][:1]), inclusive[1][:-1]], axis=0)
    returned = lax.all_to_all(
        as_sent(shifted), "ctx", split_axis=0, concat_axis=1, tiled=True
    ).astype(shifted.dtype)
    return returned.reshape(heads, hdim, hdim)


def memory_readout(
    queries_in, keys_in, incoming_values, running_decay, entering_state, query_scale
):
    count_rows = queries_in.shape[0]
    heads = queries_in.shape[1]
    hdim = queries_in.shape[2]
    width = math.gcd(heads, 8)
    causal = jnp.arange(count_rows)[:, None] >= jnp.arange(count_rows)[None, :]

    def one_group(index, result):
        start = index * width
        query_group_rows = lax.dynamic_slice_in_dim(queries_in, start, width, 1)
        group_key = lax.dynamic_slice_in_dim(keys_in, start, width, 1)
        group_value = lax.dynamic_slice_in_dim(incoming_values, start, width, 1)
        group_cumul = lax.dynamic_slice_in_dim(running_decay, start, width, 1)
        group_state = lax.dynamic_slice_in_dim(entering_state, start, width, 0)
        head_cumul = group_cumul.T
        masked = jnp.where(causal, head_cumul[:, :, None] - head_cumul[:, None, :], -jnp.inf)
        scores = jnp.einsum(
            "ihd,jhd->hij", query_group_rows, group_key, preferred_element_type=jnp.float32
        )
        weights = (jnp.exp(masked) * scores * query_scale).astype(jnp.bfloat16)
        intra = jnp.einsum("hij,jhd->ihd", weights, group_value, preferred_element_type=jnp.float32)
        upper_state_part, lower_state_part = split_parts(group_state)
        across_block_output = jnp.einsum(
            "epm,pmx->epx", query_group_rows, upper_state_part, preferred_element_type=jnp.float32
        )
        across_block_output = across_block_output + jnp.einsum(
            "epm,pmx->epx", query_group_rows, lower_state_part, preferred_element_type=jnp.float32
        )
        across_block_output = across_block_output * (jnp.exp(group_cumul) * query_scale)[:, :, None]
        group_out = (intra + across_block_output).astype(jnp.bfloat16)
        return lax.dynamic_update_slice_in_dim(result, group_out, start, 1)

    return lax.fori_loop(
        0, heads // width, one_group, jnp.zeros((count_rows, heads, hdim), jnp.bfloat16)
    )


def shards(queries, keys, values, log_decay, routes, route_weight, gain):
    tokens_here = queries.shape[1]
    heads = queries.shape[2]
    hdim = queries.shape[3]
    memories = lax.axis_size("mem")
    capacity = 2 * tokens_here // memories + tokens_here // 16
    query_scale = hdim ** (-0.5)
    local_routes = routes[0]
    member = jnp.any(
        local_routes[:, :, None] == jnp.arange(memories, dtype=jnp.int32)[None, None, :], axis=1
    )
    counted = member.astype(jnp.int32)
    rank = jnp.cumsum(counted, axis=0) - counted
    match = member[None, :, :] & (
        rank[None, :, :] == jnp.arange(capacity, dtype=jnp.int32)[:, None, None]
    )
    source = jnp.sum(
        jnp.where(match, jnp.arange(tokens_here, dtype=jnp.int32)[None, :, None], 0), axis=1
    ).T.reshape(-1)
    filled = jnp.any(match, axis=1).T.reshape(-1)

    def packed(table):
        shaped = filled.reshape((-1,) + (1,) * (table.ndim - 1))
        rows_out = jnp.where(shaped, table[source], jnp.zeros((), table.dtype))
        return rows_out.reshape((memories, capacity) + table.shape[1:])

    query_send = packed(queries[0])
    key_send = packed(keys[0])
    value_send = packed(values[0])
    rate_send = packed(log_decay[0])
    count_rows = memories * capacity
    query_got, key_got, value_got, rate_got = (
        lax.all_to_all(query_send, "mem", split_axis=0, concat_axis=0, tiled=True),
        lax.all_to_all(key_send, "mem", split_axis=0, concat_axis=0, tiled=True),
        lax.all_to_all(value_send, "mem", split_axis=0, concat_axis=0, tiled=True),
        lax.all_to_all(rate_send, "mem", split_axis=0, concat_axis=0, tiled=True),
    )
    running_decay, decay_total, state_increment = local_terms(
        key_got.reshape(count_rows, heads, hdim),
        value_got.reshape(count_rows, heads, hdim),
        rate_got.reshape(count_rows, heads),
    )
    entering_state = incoming_state(decay_total, state_increment)
    readout = memory_readout(
        query_got.reshape(count_rows, heads, hdim),
        key_got.reshape(count_rows, heads, hdim),
        value_got.reshape(count_rows, heads, hdim),
        running_decay,
        entering_state,
        query_scale,
    )
    returned = lax.all_to_all(
        readout.reshape(memories, capacity, heads, hdim),
        "mem",
        split_axis=0,
        concat_axis=0,
        tiled=True,
    )
    flat = returned.reshape(count_rows, heads, hdim)
    picked_rank = jnp.take_along_axis(rank, local_routes, axis=1)
    slot_index = local_routes * capacity + picked_rank
    first_out = head_norm(flat[slot_index[:, 0]].astype(jnp.float32))
    second_out = head_norm(flat[slot_index[:, 1]].astype(jnp.float32))
    local_weight = route_weight[0]
    mixed = first_out * local_weight[:, 0, None, None] + second_out * local_weight[:, 1, None, None]
    return (mixed * gain.reshape(heads, hdim)).astype(jnp.bfloat16)[None]


def solution(mesh):
    return jax.shard_map(
        shards,
        mesh=mesh,
        in_specs=(
            P("ctx", "mem", None, None),
            P("ctx", "mem", None, None),
            P("ctx", "mem", None, None),
            P("ctx", "mem", None),
            P("ctx", "mem", None),
            P("ctx", "mem", None),
            P(),
        ),
        out_specs=P("ctx", "mem", None, None),
        check_vma=False,
    )
```

profile of v0, /device:TPU:0, one launch (start us, length us, event | category | flops | bytes accessed | tf_op | source)
XLA Modules:
  0.0 320.2 jit_solution(15708882655729172114)
XLA Ops:
  4.7 4.3 %all-to-all-start.1 = ((bf16[4,72,32]{1,2,0:T(8,128)(2,1)}), bf16[4,72,32]{1,2,0:T(8,128)(2,1)}, u32[]{:S(2)}, u32[]{:S(2)}) async-start(bf16[4,72,32]{1,2,0:T(8,128)(2,1)} %broadcast_select_fusion.3), calls=%async_computation.1 | async-start | bytes 65536 | tf_op jit(solution)/shard_map/all_to_all | solution.py:150
  11.3 3.7 %gather_fusion.2 = bf16[288,32,128]{2,1,0:T(8,128)(2,1)} fusion(bf16[128,32,128]{2,1,0:T(8,128)(2,1)} %bitcast.123, s32[1024]{0:T(1024)S(1)} %pad_clamp_fusion.2), kind=kCustom, calls=%fused_computation.2 | custom fusion | bytes 4719744 | tf_op jit(solution)/shard_map/gather | solution.py:138
  18.0 4.1 %broadcast_select_fusion = (bf16[4,72,32,128]{3,2,1,0:T(8,128)(2,1)S(1)}, bf16[4,72,32,128]{3,2,1,0:T(8,128)(2,1)}, bf16[4,72,32,128]{3,2,1,0:T(8,128)(2,1)}) fusion(bf16[4,72,32,128]{3,2,1,0:T(8,128)(2,1)S(1)} %bitcast.117, pred[4,72]{1,0:T(4,128)(4,1)S(1)} %bitcast.141, bf16[4,72,32,128]{3,2,1,0:T(8,128)(2,1)} %bitcast.118, ...), kind=kLoop, calls=%fused_computation.45 | loop fusion | flops 3538944 | bytes 14156064 | tf_op jit(solution)/shard_map/jit(_where)/select_n | solution.py:138
  24.4 3.9 %all-to-all-start.3 = ((bf16[4,72,32,128]{3,1,2,0:T(8,128)(2,1)}), bf16[4,72,32,128]{3,1,2,0:T(8,128)(2,1)S(1)}, u32[]{:S(2)}, u32[]{:S(2)}) async-start(bf16[4,72,32,128]{3,1,2,0:T(8,128)(2,1)} %copy.91), calls=%async_computation.3 | async-start | bytes 4718592 | tf_op jit(solution)/shard_map/all_to_all | solution.py:148
  28.3 4.0 %copy.82 = bf16[4,72,32,128]{3,1,2,0:T(8,128)(2,1)} copy(bf16[4,72,32,128]{3,2,1,0:T(8,128)(2,1)} %get-tuple-element.207) | data formatting | bytes 4718592 | tf_op jit(solution)/shard_map/jit(_where)/select_n | solution.py:138
  32.3 24.5 %all-to-all-done.3 = bf16[4,72,32,128]{3,1,2,0:T(8,128)(2,1)S(1)} async-done(((bf16[4,72,32,128]{3,1,2,0:T(8,128)(2,1)}), bf16[4,72,32,128]{3,1,2,0:T(8,128)(2,1)S(1)}, u32[]{:S(2)}, u32[]{:S(2)}) %all-to-all-start.3) | async-done | bytes 2359328 | tf_op jit(solution)/shard_map/all_to_all | solution.py:148
  56.8 4.5 %all-to-all-start = ((bf16[4,72,32,128]{3,1,2,0:T(8,128)(2,1)}), bf16[4,72,32,128]{3,1,2,0:T(8,128)(2,1)}, u32[]{:S(2)}, u32[]{:S(2)}) async-start(bf16[4,72,32,128]{3,1,2,0:T(8,128)(2,1)} %copy.82), calls=%async_computation | async-start | bytes 4718592 | tf_op jit(solution)/shard_map/all_to_all | solution.py:149
  68.4 4.5 %fusion.20 = (bf16[288,32,128]{2,1,0:T(8,128)(2,1)}, bf16[288,32,128]{2,1,0:T(8,128)(2,1)S(1)}) fusion(f32[288,32]{1,0:T(8,128)S(1)} %copy.93, bf16[4,72,32,128]{3,2,1,0:T(8,128)(2,1)} %copy.92), kind=kLoop, calls=%fused_computation.36 | loop fusion | flops 7077888 | bytes 7114752 | tf_op jit(solution)/shard_map/convert_element_type | solution.py:18
  72.8 17.0 %all-to-all-done = bf16[4,72,32,128]{3,1,2,0:T(8,128)(2,1)} async-done(((bf16[4,72,32,128]{3,1,2,0:T(8,128)(2,1)}), bf16[4,72,32,128]{3,1,2,0:T(8,128)(2,1)}, u32[]{:S(2)}, u32[]{:S(2)}) %all-to-all-start) | async-done | bytes 2359328 | tf_op jit(solution)/shard_map/all_to_all | solution.py:149
  89.9 6.6 %all-to-all-start.5 = ((bf16[8,2,256]{2,1,0:T(2,128)(2,1)}), bf16[8,2,256]{2,1,0:T(2,128)(2,1)S(1)}, u32[]{:S(2)}, u32[]{:S(2)}) async-start(bf16[8,2,256]{2,1,0:T(2,128)(2,1)} %reshape.334), calls=%async_computation.5 | async-start | bytes 16384 | tf_op jit(solution)/shard_map/all_to_all | solution.py:60
  103.2 16.7 %copy.131 = bf16[1,4096,128]{2,0,1:T(2,128)(2,1)S(1)} copy(bf16[1,4096,128]{2,1,0:T(8,128)(2,1)S(1)} %bitcast.125) | data formatting | bytes 2097152 | tf_op jit(solution)/shard_map/convert_element_type | solution.py:54
  119.9 22.4 %reduce.12 = bf16[4096,128]{1,0:T(8,128)(2,1)S(1)} reduce(bf16[4096,1,128]{2,1,0:T(2,128)(2,1)S(1)} %bitcast.122, bf16[]{:T(256)} %broadcast.245), dimensions={1}, to_apply=%bitcast.100.reduce_sub_computation | reduce | bytes 2097154
  143.4 6.0 %all-to-all-start.4 = ((bf16[8,2,32768]{2,1,0:T(2,128)(2,1)}), bf16[8,2,32768]{2,1,0:T(2,128)(2,1)S(1)}, u32[]{:S(2)}, u32[]{:S(2)}) async-start(bf16[8,2,32768]{2,1,0:T(2,128)(2,1)} %reshape.332), calls=%async_computation.4 | async-start | bytes 2097152 | tf_op jit(solution)/shard_map/all_to_all | solution.py:53
  152.0 22.6 %all-to-all-done.4 = bf16[8,2,32768]{2,1,0:T(2,128)(2,1)S(1)} async-done(((bf16[8,2,32768]{2,1,0:T(2,128)(2,1)}), bf16[8,2,32768]{2,1,0:T(2,128)(2,1)S(1)}, u32[]{:S(2)}, u32[]{:S(2)}) %all-to-all-start.4) | async-done | bytes 1048608 | tf_op jit(solution)/shard_map/all_to_all | solution.py:53
  174.6 4.7 %all-to-all-start.2 = ((bf16[4,72,32,128]{3,1,2,0:T(8,128)(2,1)}), bf16[4,72,32,128]{3,1,2,0:T(8,128)(2,1)}, u32[]{:S(2)}, u32[]{:S(2)}) async-start(bf16[4,72,32,128]{3,1,2,0:T(8,128)(2,1)} %copy.89), calls=%async_computation.2 | async-start | bytes 4718592 | tf_op jit(solution)/shard_map/all_to_all | solution.py:147
  179.3 3.5 %reshape.333 = bf16[4096,1,128]{2,1,0:T(2,128)(2,1)} reshape(bf16[8,2,32768]{2,1,0:T(2,128)(2,1)S(1)} %all-to-all-done.4) | data formatting | bytes 2097152
  182.7 3.8 %bitcast_convert_fusion.1 = f32[1,4096,128]{2,0,1:T(1,128)S(1)} fusion(bf16[4096,1,128]{2,1,0:T(2,128)(2,1)} %reshape.333), kind=kLoop, calls=%fused_computation.114 | loop fusion | flops 524288 | bytes 3145728 | tf_op jit(solution)/shard_map/convert_element_type | solution.py:59
  207.6 3.6 %all-to-all-start.6 = ((bf16[8,512,128]{2,1,0:T(8,128)(2,1)}), bf16[8,512,128]{2,1,0:T(8,128)(2,1)S(1)}, u32[]{:S(2)}, u32[]{:S(2)}) async-start(bf16[8,512,128]{2,1,0:T(8,128)(2,1)} %concatenate.11), calls=%async_computation.6 | async-start | bytes 2097152 | tf_op jit(solution)/shard_map/all_to_all | solution.py:70
  211.2 3.6 %copy.90 = bf16[4,72,32,128]{3,2,1,0:T(8,128)(2,1)} copy(bf16[4,72,32,128]{3,1,2,0:T(8,128)(2,1)} %all-to-all-done.2) | data formatting | bytes 4718592 | tf_op jit(solution)/shard_map/all_to_all | solution.py:147
  214.7 22.1 %all-to-all-done.6 = bf16[8,512,128]{2,1,0:T(8,128)(2,1)S(1)} async-done(((bf16[8,512,128]{2,1,0:T(8,128)(2,1)}), bf16[8,512,128]{2,1,0:T(8,128)(2,1)S(1)}, u32[]{:S(2)}, u32[]{:S(2)}) %all-to-all-start.6) | async-done | bytes 1048608 | tf_op jit(solution)/shard_map/all_to_all | solution.py:70
  240.2 33.5 %while.14 = (s32[]{:T(128)}, bf16[288,32,128]{2,0,1:T(8,128)(2,1)}, bf16[288,32,128]{2,0,1:T(8,128)(2,1)}, f32[288,32]{0,1:T(8,128)}, bf16[288,32,128]{2,1,0:T(8...) while((s32[]{:T(128)}, bf16[288,32,128]{2,0,1:T(8,128)(2,1)}, ...), condition=%wide.region_7.8_spmd.clone, body=%wide.region_6.7_spmd.clone.sunk | while | flops 495840512 | bytes 11659435 | solution.py:110
  273.7 4.0 %copy.102 = bf16[4,72,32,128]{3,2,1,0:T(8,128)(2,1)} copy(bf16[4,72,32,128]{3,1,0,2:T(8,128)(2,1)} %bitcast.116) | data formatting | bytes 4718592 | tf_op jit(solution)/shard_map/reshape | solution.py:167
  277.7 3.8 %all-to-all-start.7 = ((bf16[4,72,32,128]{3,2,1,0:T(8,128)(2,1)}), bf16[4,72,32,128]{3,2,1,0:T(8,128)(2,1)S(1)}, u32[]{:S(2)}, u32[]{:S(2)}) async-start(bf16[4,72,32,128]{3,2,1,0:T(8,128)(2,1)} %copy.102), calls=%async_computation.7 | async-start | bytes 4718592 | tf_op jit(solution)/shard_map/all_to_all | solution.py:166
  284.1 25.8 %all-to-all-done.7 = bf16[4,72,32,128]{3,2,1,0:T(8,128)(2,1)S(1)} async-done(((bf16[4,72,32,128]{3,2,1,0:T(8,128)(2,1)}), bf16[4,72,32,128]{3,2,1,0:T(8,128)(2,1)S(1)}, u32[]{:S(2)}, u32[]{:S(2)}) %all-to-all-start.7) | async-done | bytes 2359328 | tf_op jit(solution)/shard_map/all_to_all | solution.py:166
  (144 shorter events, 100.2 us)
Async XLA Ops:
  0.0 9.0 %copy-start = (bf16[1,128,32,128]{3,2,1,0:T(8,128)(2,1)S(1)}, bf16[1,128,32,128]{3,2,1,0:T(8,128)(2,1)}, u32[]{:S(2)}) copy-start(bf16[1,128,32,128]{3,2,1,0:T(8,128)(2,1)} %param.10) | copy-start | bytes 3145732
  4.7 19.7 %all-to-all-start.1 = ((bf16[4,72,32]{1,2,0:T(8,128)(2,1)}), bf16[4,72,32]{1,2,0:T(8,128)(2,1)}, u32[]{:S(2)}, u32[]{:S(2)}) async-start(bf16[4,72,32]{1,2,0:T(8,128)(2,1)} %broadcast_select_fusion.3), calls=%async_computation.1 | async-start | bytes 65536 | tf_op jit(solution)/shard_map/all_to_all | solution.py:150
  11.3 3.7 %copy-start.7 = (bf16[1,128,32,128]{3,2,1,0:T(8,128)(2,1)S(1)}, bf16[1,128,32,128]{3,2,1,0:T(8,128)(2,1)}, u32[]{:S(2)}) copy-start(bf16[1,128,32,128]{3,2,1,0:T(8,128)(2,1)} %param.11) | copy-start | bytes 3145732
  24.4 32.4 %all-to-all-start.3 = ((bf16[4,72,32,128]{3,1,2,0:T(8,128)(2,1)}), bf16[4,72,32,128]{3,1,2,0:T(8,128)(2,1)S(1)}, u32[]{:S(2)}, u32[]{:S(2)}) async-start(bf16[4,72,32,128]{3,1,2,0:T(8,128)(2,1)} %copy.91), calls=%async_computation.3 | async-start | bytes 4718592 | tf_op jit(solution)/shard_map/all_to_all | solution.py:148
  56.8 33.0 %all-to-all-start = ((bf16[4,72,32,128]{3,1,2,0:T(8,128)(2,1)}), bf16[4,72,32,128]{3,1,2,0:T(8,128)(2,1)}, u32[]{:S(2)}, u32[]{:S(2)}) async-start(bf16[4,72,32,128]{3,1,2,0:T(8,128)(2,1)} %copy.82), calls=%async_computation | async-start | bytes 4718592 | tf_op jit(solution)/shard_map/all_to_all | solution.py:149
  89.9 53.6 %all-to-all-start.5 = ((bf16[8,2,256]{2,1,0:T(2,128)(2,1)}), bf16[8,2,256]{2,1,0:T(2,128)(2,1)S(1)}, u32[]{:S(2)}, u32[]{:S(2)}) async-start(bf16[8,2,256]{2,1,0:T(2,128)(2,1)} %reshape.334), calls=%async_computation.5 | async-start | bytes 16384 | tf_op jit(solution)/shard_map/all_to_all | solution.py:60
  98.3 2.2 copy-start.2
  98.3 2.5 copy-start.3
  142.3 7.1 %copy-start.4 = (bf16[4,72,32,128]{3,2,1,0:T(8,128)(2,1)S(1)}, bf16[4,72,32,128]{3,2,1,0:T(8,128)(2,1)}, u32[]{:S(2)}) copy-start(bf16[4,72,32,128]{3,2,1,0:T(8,128)(2,1)} %get-tuple-element.206) | copy-start | bytes 7077892
  143.4 31.1 %all-to-all-start.4 = ((bf16[8,2,32768]{2,1,0:T(2,128)(2,1)}), bf16[8,2,32768]{2,1,0:T(2,128)(2,1)S(1)}, u32[]{:S(2)}, u32[]{:S(2)}) async-start(bf16[8,2,32768]{2,1,0:T(2,128)(2,1)} %reshape.332), calls=%async_computation.4 | async-start | bytes 2097152 | tf_op jit(solution)/shard_map/all_to_all | solution.py:53
  174.6 33.0 %all-to-all-start.2 = ((bf16[4,72,32,128]{3,1,2,0:T(8,128)(2,1)}), bf16[4,72,32,128]{3,1,2,0:T(8,128)(2,1)}, u32[]{:S(2)}, u32[]{:S(2)}) async-start(bf16[4,72,32,128]{3,1,2,0:T(8,128)(2,1)} %copy.89), calls=%async_computation.2 | async-start | bytes 4718592 | tf_op jit(solution)/shard_map/all_to_all | solution.py:147
  189.1 0.7 copy-start.9
  196.3 2.4 copy-start.6
  198.7 1.0 copy-start.10
  199.6 2.9 copy-start.8
  207.6 29.2 %all-to-all-start.6 = ((bf16[8,512,128]{2,1,0:T(8,128)(2,1)}), bf16[8,512,128]{2,1,0:T(8,128)(2,1)S(1)}, u32[]{:S(2)}, u32[]{:S(2)}) async-start(bf16[8,512,128]{2,1,0:T(8,128)(2,1)} %concatenate.11), calls=%async_computation.6 | async-start | bytes 2097152 | tf_op jit(solution)/shard_map/all_to_all | solution.py:70
  277.7 3.8 %copy-start.12 = (s32[1,128,2]{1,2,0:T(2,128)S(1)}, s32[1,128,2]{1,2,0:T(2,128)}, u32[]{:S(2)}) copy-start(s32[1,128,2]{1,2,0:T(2,128)} %param.13) | copy-start | bytes 3076
  277.7 32.2 %all-to-all-start.7 = ((bf16[4,72,32,128]{3,2,1,0:T(8,128)(2,1)}), bf16[4,72,32,128]{3,2,1,0:T(8,128)(2,1)S(1)}, u32[]{:S(2)}, u32[]{:S(2)}) async-start(bf16[4,72,32,128]{3,2,1,0:T(8,128)(2,1)} %copy.102), calls=%async_computation.7 | async-start | bytes 4718592 | tf_op jit(solution)/shard_map/all_to_all | solution.py:166
  281.7 2.3 copy-start.13
  309.9 1.4 copy-start.5
  313.7 3.7 %copy-start.11 = (f32[4096]{0:T(1024)S(1)}, f32[4096]{0:T(1024)}, u32[]{:S(2)}) copy-start(f32[4096]{0:T(1024)} %param.15) | copy-start | bytes 49156
  316.2 4.0 %copy-start.1 = (bf16[1,128,32,128]{3,2,1,0:T(8,128)(2,1)S(1)}, bf16[1,128,32,128]{3,2,1,0:T(8,128)(2,1)}, u32[]{:S(2)}) copy-start(bf16[1,128,32,128]{3,2,1,0:T(8,128)(2,1)} %param.10) | copy-start | bytes 3145732
where the time goes:
time: 322 us; the launch traced here: 320 us
  waiting for transfers between devices  114 us (35%)
  local copies, waits for them, and re-layouts  83.6 us (26%)
  other arithmetic  55 us (17%)
  starting transfers between devices  37.3 us (12%)
  matrix products  29.6 us (9%)
    all_to_all x1, waiting for transfers between devices, shards(): lax.all_to_all(readout.reshape(memories, capacity, heads, hdim), 'mem', s...  25.8 us
    all_to_all x1, waiting for transfers between devices, shards(): lax.all_to_all(key_send, 'mem', split_axis=0, concat_axis=0, tiled=True)  24.5 us
    unnamed x2, other arithmetic  23.1 us
    all_to_all x1, waiting for transfers between devices, incoming_state(): lax.all_to_all(state_increment.reshape(1, flat_rows, hdim).astype(jnp.bfl...  22.6 us
    all_to_all x1, waiting for transfers between devices, incoming_state(): lax.all_to_all(as_sent(shifted), 'ctx', split_axis=0, concat_axis=1, tile...  22.1 us
    all_to_all x1, waiting for transfers between devices, shards(): lax.all_to_all(value_send, 'mem', split_axis=0, concat_axis=0, tiled=True)  17 us
    convert_element_type x1, local copies, waits for them, and re-layouts, incoming_state(): state_increment.reshape(1, flat_rows, hdim).astype(jnp.bfloat16)  16.7 us
    unnamed x37, local copies, waits for them, and re-layouts  10.6 us
  transfers between devices with their start and end apart: 8, of which 6 were waited for; matrix products, arithmetic and copies ran while one was open for 35% of the time, Pallas kernels for 0%

commit v1 on v0

v1 whole, which is shorter than its diff:
```python
import functools

import jax
import jax.numpy as jnp
from jax import lax
from jax.experimental import pallas as pl
from jax.experimental.pallas import tpu as pltpu
from jax.sharding import Mesh
from jax.sharding import PartitionSpec as P

F32 = jnp.float32
BF16 = jnp.bfloat16
META = 16
ROWS = 8


def dot(a, b, dims=((1,), (0,))):
    return lax.dot_general(a, b, (dims, ((), ())), preferred_element_type=F32)


def pack_kernel(hl, td, q_ref, k_ref, v_ref, ld_ref, rt_ref, wt_ref, kv_out, q_out, scr, ld_scr):
    i = pl.program_id(0)
    hb = q_ref.shape[1]
    hd = q_ref.shape[2]

    @pl.when(i == 0)
    def _():
        ld_scr[...] = ld_ref[...].astype(F32)

    for src, out, base in ((k_ref, kv_out, 0), (v_ref, kv_out, hl * td), (q_ref, q_out, 0)):
        scr[...] = src[...].astype(F32).reshape(td * hb, hd)
        for j in range(hb):
            rows = scr[pl.ds(j, td, stride=hb), :].astype(BF16)
            start = base + (j % hl) * td
            out[j // hl, start : start + td, :] = rows
    w = wt_ref[...]
    hi = w.astype(BF16).astype(F32)
    mid = (w - hi).astype(BF16).astype(F32)
    low = (w - hi) - mid
    table = jnp.concatenate([rt_ref[...].astype(F32), hi, mid, low], axis=0)
    here = ld_scr[pl.ds(pl.multiple_of(i * hb, hb), hb), :]
    for dd in range(hb // hl):
        own = here if dd == 0 else pltpu.roll(here, hb - dd * hl, 0)
        kv_out[dd, 2 * hl * td :, :] = jnp.concatenate([table, own], axis=0).astype(BF16)


def pack(queries, keys, values, ld_t, routes_t, weight_t, g, hl):
    td, heads, hd = queries.shape
    hb = 8
    per = hb // hl
    rows = 2 * hl * td + META
    whole = lambda a: pl.BlockSpec(a.shape, lambda i: (0,) * a.ndim)
    block = pl.BlockSpec((td, hb, hd), lambda i: (0, i, 0))
    return pl.pallas_call(
        functools.partial(pack_kernel, hl, td),
        grid=(heads // hb,),
        in_specs=[block, block, block, whole(ld_t), whole(routes_t), whole(weight_t)],
        out_specs=[
            pl.BlockSpec((per, rows, hd), lambda i: (i, 0, 0)),
            pl.BlockSpec((per, hl * td, hd), lambda i: (i, 0, 0)),
        ],
        out_shape=[
            jax.ShapeDtypeStruct((g, rows, hd), BF16),
            jax.ShapeDtypeStruct((g, hl * td, hd), BF16),
        ],
        scratch_shapes=[pltpu.VMEM((td * hb, hd), F32), pltpu.VMEM((heads, td), F32)],
        name="pack",
    )(queries, keys, values, ld_t, routes_t, weight_t)


def meta_rows(kv_ref, s, hl, memories, base):
    meta = kv_ref[s, base:, :].astype(F32)
    td = meta.shape[1]
    row = lax.broadcasted_iota(jnp.int32, (ROWS, td), 0)
    memory = lax.rem(row, memories).astype(F32)
    first = meta[0:1] == memory
    second = meta[1:2] == memory
    rate = jnp.broadcast_to(meta[8:9], (ROWS, td))
    for h in range(1, hl):
        rate = jnp.where(row >= h * memories, meta[8 + h : 9 + h], rate)
    member = first | second
    return meta, first, second, member, jnp.where(member, rate, 0.0)


def running_sums(kv_ref, a_scr, cs_scr, g, hl, memories, base):
    td = a_scr.shape[1]
    for s in range(g):
        a_scr[s * ROWS : (s + 1) * ROWS, :] = meta_rows(kv_ref, s, hl, memories, base)[4]
    t0 = lax.broadcasted_iota(jnp.int32, (td, 2 * td), 0)
    t1 = lax.broadcasted_iota(jnp.int32, (td, 2 * td), 1)
    upper = jnp.where(t0 <= t1, 1.0, 0.0).astype(BF16)
    cs_scr[...] = dot(a_scr[...].astype(BF16), upper)


def state_kernel(g, hl, memories, td, kv_ref, state_ref, total_ref, a_scr, cs_scr, dec_scr, acc_scr):
    hd = kv_ref.shape[2]
    base = 2 * hl * td
    running_sums(kv_ref, a_scr, cs_scr, g, hl, memories, base)
    after = jnp.zeros((ROWS, td), F32)
    for s in reversed(range(g)):
        member = meta_rows(kv_ref, s, hl, memories, base)[3]
        rows = slice(s * ROWS, (s + 1) * ROWS)
        running, total = cs_scr[rows, :td], cs_scr[rows, td:]
        dec_scr[s] = jnp.where(member, jnp.exp(total - running + after), 0.0)
        after = after + total
    total_ref[...] = jnp.exp(after)
    acc_scr[...] = jnp.zeros_like(acc_scr)

    def chunk(s, carry):
        columns = dec_scr[s].T
        for h in range(hl):
            key = kv_ref[s, h * td : (h + 1) * td, :]
            value = kv_ref[s, (hl + h) * td : (hl + h + 1) * td, :].astype(F32)
            scaled = jnp.concatenate(
                [
                    (value * columns[:, h * memories + m : h * memories + m + 1]).astype(BF16)
                    for m in range(memories)
                ],
                axis=1,
            )
            acc_scr[h] += dot(key, scaled, ((0,), (0,)))
        return carry

    lax.fori_loop(0, g, chunk, 0)
    state_ref[...] = acc_scr[...].astype(BF16)


def local_state(kv, hl, memories, td):
    g, rows, hd = kv.shape
    return pl.pallas_call(
        functools.partial(state_kernel, g, hl, memories, td),
        in_specs=[pl.BlockSpec(memory_space=pltpu.VMEM)],
        out_specs=[pl.BlockSpec(memory_space=pltpu.VMEM)] * 2,
        out_shape=[
            jax.ShapeDtypeStruct((hl, hd, memories * hd), BF16),
            jax.ShapeDtypeStruct((ROWS, td), F32),
        ],
        scratch_shapes=[
            pltpu.VMEM((g * ROWS, td), F32),
            pltpu.VMEM((g * ROWS, 2 * td), F32),
            pltpu.VMEM((g, ROWS, td), F32),
            pltpu.VMEM((hl, hd, memories * hd), F32),
        ],
        cost_estimate=pl.CostEstimate(
            flops=2 * g * td * hl * memories * hd * hd, bytes_accessed=kv.size * 2, transcendentals=0
        ),
        name="local_state",
    )(kv)


def readout_kernel(
    g, hl, memories, td, q_ref, kv_ref, state_ref, gain_ref, out_ref, a_scr, cs_scr, col_scr, fac_scr, st_scr
):
    hd = kv_ref.shape[2]
    base = 2 * hl * td
    scale = hd ** (-0.5)
    running_sums(kv_ref, a_scr, cs_scr, g, hl, memories, base)
    half_after = jnp.ones((ROWS, td), F32)
    for s in reversed(range(g)):
        meta, first, second, member, _ = meta_rows(kv_ref, s, hl, memories, base)
        rows = slice(s * ROWS, (s + 1) * ROWS)
        running, half = cs_scr[rows, :td], 0.5 * cs_scr[rows, td:]
        weight = [meta[2 + i : 3 + i] + (meta[4 + i : 5 + i] + meta[6 + i : 7 + i]) for i in range(2)]
        col_scr[s, 0:ROWS, :] = jnp.where(member, jnp.exp(half - running), 0.0)
        col_scr[s, ROWS : 2 * ROWS, :] = jnp.exp(running - half) * scale
        col_scr[s, 2 * ROWS :, :] = jnp.where(first, weight[0], 0.0) + jnp.where(second, weight[1], 0.0)
        own = jnp.exp(half)
        fac_scr[s, 0:ROWS, :] = own
        fac_scr[s, ROWS:, :] = half_after
        half_after = own
    for h in range(hl):
        for m in range(memories):
            j = h * memories + m
            lanes = slice(m * hd, (m + 1) * hd)
            st_scr[h, :, lanes] = state_ref[h, :, lanes].astype(F32) * half_after[j : j + 1, :]
    ones = jnp.full((hd, hd), 1.0 / hd, F32).astype(BF16)
    causal = lax.broadcasted_iota(jnp.int32, (td, td), 0) >= lax.broadcasted_iota(jnp.int32, (td, td), 1)

    def chunk(s, carry):
        columns = col_scr[s].T
        factors = fac_scr[s]
        for h in range(hl):
            query = q_ref[s, h * td : (h + 1) * td, :]
            key = kv_ref[s, h * td : (h + 1) * td, :]
            value = kv_ref[s, (hl + h) * td : (hl + h + 1) * td, :].astype(F32)
            scores = jnp.where(causal, dot(query, key, ((1,), (1,))), 0.0).astype(BF16)
            scaled = jnp.concatenate(
                [
                    (value * columns[:, h * memories + m : h * memories + m + 1]).astype(BF16)
                    for m in range(memories)
                ],
                axis=1,
            )
            state = st_scr[h]
            left = jnp.concatenate([scores, query], axis=1)
            right = jnp.concatenate([scaled, state.astype(BF16)], axis=0)
            read = dot(left, right)
            grown = state + dot(key, scaled, ((0,), (0,)))
            mixed = jnp.zeros((td, hd), F32)
            for m in range(memories):
                j = h * memories + m
                lanes = slice(m * hd, (m + 1) * hd)
                st_scr[h, :, lanes] = (
                    grown[:, lanes] * factors[j : j + 1, :] * factors[ROWS + j : ROWS + j + 1, :]
                )
                rows_out = read[:, lanes] * columns[:, ROWS + j : ROWS + j + 1]
                mean = dot((rows_out * rows_out).astype(BF16), ones)
                mixed = mixed + rows_out * (
                    lax.rsqrt(mean + 1e-06) * columns[:, 2 * ROWS + j : 2 * ROWS + j + 1]
                )
            out_ref[s, h * td : (h + 1) * td, :] = (mixed * gain_ref[h : h + 1, :]).astype(BF16)
        return carry

    lax.fori_loop(0, g, chunk, 0)


def readout(q, kv, state, gain, hl, memories, td):
    g, rows, hd = kv.shape
    return pl.pallas_call(
        functools.partial(readout_kernel, g, hl, memories, td),
        in_specs=[pl.BlockSpec(memory_space=pltpu.VMEM)] * 4,
        out_specs=pl.BlockSpec(memory_space=pltpu.VMEM),
        out_shape=jax.ShapeDtypeStruct(q.shape, BF16),
        scratch_shapes=[
            pltpu.VMEM((g * ROWS, td), F32),
            pltpu.VMEM((g * ROWS, 2 * td), F32),
            pltpu.VMEM((g, 3 * ROWS, td), F32),
            pltpu.VMEM((g, 2 * ROWS, td), F32),
            pltpu.VMEM((hl, hd, memories * hd), F32),
        ],
        cost_estimate=pl.CostEstimate(
            flops=8 * g * td * hl * memories * hd * hd, bytes_accessed=kv.size * 4, transcendentals=0
        ),
        name="readout",
    )(q, kv, state, gain)


def entering_state(state, total, groups, hl, memories):
    if groups == 1:
        return jnp.zeros_like(state)
    state = lax.ppermute(state, "hi", [(i, i + 1) for i in range(groups - 1)])
    if groups == 2:
        return state
    factor = lax.ppermute(total[:, :1], "hi", [(i, i + 1) for i in range(groups - 1)])

    def spread(f):
        shaped = f.reshape(hl, 1, memories, 1)
        wide = jnp.broadcast_to(shaped, (hl, 1, memories, state.shape[1]))
        return wide.reshape(hl, 1, state.shape[2])

    held = state.astype(F32)
    step = 1
    while step < groups - 1:
        pairs = [(i, i + step) for i in range(groups - step)]
        earlier = lax.ppermute(held.astype(BF16), "hi", pairs).astype(F32)
        earlier_factor = lax.ppermute(factor, "hi", pairs)
        held = held + spread(factor) * earlier
        factor = factor * earlier_factor
        step *= 2
    return held.astype(BF16)


def shards(queries, keys, values, log_decay, routes, route_weight, gain):
    td, heads, hd = queries.shape[1:]
    memories = lax.axis_size("mem")
    lo = lax.axis_size("lo")
    groups = lax.axis_size("hi")
    g = memories * lo
    hl = heads // g
    axes = ("lo", "mem")
    kv_send, q_send = pack(
        queries[0], keys[0], values[0], log_decay[0].T, routes[0].T, route_weight[0].T, g, hl
    )
    kv = lax.all_to_all(kv_send, axes, split_axis=0, concat_axis=0, tiled=True)
    q = lax.all_to_all(q_send, axes, split_axis=0, concat_axis=0, tiled=True)
    state, total = local_state(kv, hl, memories, td)
    entering = entering_state(state, total, groups, hl, memories)
    place = lax.axis_index("lo") * memories + lax.axis_index("mem")
    own_gain = lax.dynamic_slice_in_dim(gain.reshape(heads, hd), place * hl, hl, 0)
    out = readout(q, kv, entering, own_gain, hl, memories, td)
    back = lax.all_to_all(out, axes, split_axis=0, concat_axis=0, tiled=True)
    return back.reshape(heads, td, hd).transpose(1, 0, 2)[None]


def solution(mesh):
    memories, blocks = mesh.shape["mem"], mesh.shape["ctx"]
    def call(queries, keys, values, log_decay, routes, route_weight, gain):
        heads = queries.shape[2]
        lo = max(
            s
            for s in range(1, max(1, blocks // 2) + 1)
            if blocks % s == 0 and heads % (memories * s) == 0
        )
        split = Mesh(mesh.devices.reshape(memories, blocks // lo, lo), ("mem", "hi", "lo"))
        tokens = P(("hi", "lo"), "mem")
        return jax.shard_map(
            shards,
            mesh=split,
            in_specs=(tokens,) * 6 + (P(),),
            out_specs=tokens,
            check_vma=False,
        )(queries, keys, values, log_decay, routes, route_weight, gain)

    return call
```

time: 322 us -> 112 us (0.35)
  waiting for transfers between devices: 114 us -> 5.75 us
  local copies, waits for them, and re-layouts: 83.6 us -> 2.94 us
  blocking collectives: 0 us -> 61.1 us
  other arithmetic: 55 us -> 0 us
  Pallas kernels: 0 us -> 33.1 us
  matrix products: 29.6 us -> 0 us
  starting transfers between devices: 37.3 us -> 8.15 us
    all_to_all x8 -> x1, waiting for transfers between devices: 114 us -> 0.43 us  [shards(): q = lax.all_to_all(q_send, axes, split_axis=0, concat_axis=0, tiled=True)]
    all_to_all x0 -> x2, blocking collectives: none -> 61.1 us  [the longest x1 34.5 us: shards(): kv = lax.all_to_all(kv_send, axes, split_axis=0, concat_axis=0, tiled=True)]
    all_to_all x8 -> x1, starting transfers between devices: 37.3 us -> 3.66 us  [shards(): q = lax.all_to_all(q_send, axes, split_axis=0, concat_axis=0, tiled=True)]
    pallas_call x0 -> x3, Pallas kernels: none -> 33.1 us  [the longest x1 17.6 us: readout(): pl.pallas_call(functools.partial(readout_kernel, g, hl, memories, td), in...]
    dot_general x14 -> x0, matrix products: 29.6 us -> none  [the longest x4 10.2 us: one_group(): jnp.einsum('hij,jhd->ihd', weights, group_value, preferred_element_type=j...]
    unnamed x2 -> x0, other arithmetic: 23.1 us -> none
    gather x11 -> x0, local copies, waits for them, and re-layouts: 17.6 us -> none  [the longest x5 10.4 us: packed(): rows_out = jnp.where(shaped, table[source], jnp.zeros((), table.dtype))]
    convert_element_type x7 -> x0, local copies, waits for them, and re-layouts: 17.2 us -> none  [the longest x1 16.7 us: incoming_state(): state_increment.reshape(1, flat_rows, hdim).astype(jnp.bfloat16)]
  transfers between devices with their start and end apart: 8 -> 2, of which waited for: 6 -> 2; matrix products, arithmetic and copies ran while one was open for 35% -> 1% of each run, Pallas kernels for 0% -> 10%
where the time goes in v1:
time: 112 us; the launch traced here: 111 us
  blocking collectives  61.1 us (55%)
  Pallas kernels  33.1 us (30%)
  starting transfers between devices  8.15 us (7%)
  waiting for transfers between devices  5.75 us (5%)
  local copies, waits for them, and re-layouts  2.94 us (3%)
    all_to_all x1, blocking collectives, shards(): kv = lax.all_to_all(kv_send, axes, split_axis=0, concat_axis=0, tiled=True)  34.5 us
    all_to_all x1, blocking collectives, shards(): back = lax.all_to_all(out, axes, split_axis=0, concat_axis=0, tiled=True)  26.6 us
    pallas_call x1, Pallas kernels, readout(): pl.pallas_call(functools.partial(readout_kernel, g, hl, memories, td), in...  17.6 us
    pallas_call x1, Pallas kernels, local_state(): pl.pallas_call(functools.partial(state_kernel, g, hl, memories, td), in_s...  10.6 us
    ppermute x1, waiting for transfers between devices, entering_state(): state = lax.ppermute(state, 'hi', [(i, i + 1) for i in range(groups - 1)])  5.32 us
    pallas_call x1, Pallas kernels, pack(): pl.pallas_call(functools.partial(pack_kernel, hl, td), grid=(heads // hb,...  4.84 us
    ppermute x1, starting transfers between devices, entering_state(): state = lax.ppermute(state, 'hi', [(i, i + 1) for i in range(groups - 1)])  4.5 us
    all_to_all x1, starting transfers between devices, shards(): q = lax.all_to_all(q_send, axes, split_axis=0, concat_axis=0, tiled=True)  3.66 us
  transfers between devices with their start and end apart: 2, of which 2 were waited for; matrix products, arithmetic and copies ran while one was open for 1% of the time, Pallas kernels for 10%

profile of v1, /device:TPU:0, one launch (start us, length us, event | category | flops | bytes accessed | tf_op | source)
XLA Modules:
  0.0 111.0 jit_solution(14841818702623044702)
XLA Ops:
  0.0 0.0 copy-start
  0.0 4.8 %pack.1 = (bf16[16,528,128]{2,1,0:T(8,128)(2,1)}, bf16[16,256,128]{2,1,0:T(8,128)(2,1)}) custom-call(bf16[128,32,128]{2,1,0:T(8,128)(2,1)} %bitcast.21, bf16[128,32,128]{2,1,0:T(8,128)(2,1)} %bitcast.22, bf16[128,32,128]{2,1,0:T(8,128)(2,1)} %bitcast.23, bf16[32,128]{1,0:T(8,128)(2,1)} %bitcast.24, s32[2,128]{1,0:T(2,128)} %bitcast.25, f32[2,128]{1,0:T(2,128)} %bitcast.26), custom_call_target="tpu_custom_call" | custom-call | tf_op jit(solution)/shard_map/pack/pallas_call | solution.py:54
  4.8 34.5 %all_to_all.15.kv_ref = bf16[16,528,128]{2,1,0:T(8,128)(2,1)} all-to-all(bf16[16,528,128]{2,1,0:T(8,128)(2,1)} %get-tuple-element.9), channel_id=1, replica_groups=mesh['mem'=4,'hi'=2,'lo'=4] {'lo','mem'}, dimensions={0} | all-to-all | bytes 4325376 | tf_op jit(solution)/shard_map/all_to_all | solution.py:274
  39.3 3.7 %all-to-all-start = ((bf16[16,256,128]{2,1,0:T(8,128)(2,1)}), bf16[16,256,128]{2,1,0:T(8,128)(2,1)S(1)}, u32[]{:S(2)}, u32[]{:S(2)}) async-start(bf16[16,256,128]{2,1,0:T(8,128)(2,1)} %get-tuple-element.8), calls=%async_computation | async-start | bytes 2097152 | tf_op jit(solution)/shard_map/all_to_all | solution.py:275
  43.0 10.6 %local_state.1 = (bf16[2,128,512]{2,1,0:T(8,128)(2,1)}, f32[8,128]{1,0:T(8,128)}) custom-call(bf16[16,528,128]{2,1,0:T(8,128)(2,1)} %all_to_all.15.kv_ref), custom_call_target="tpu_custom_call" | custom-call | flops 536870912 | bytes 2162688 | tf_op jit(solution)/shard_map/local_state/pallas_call | solution.py:130
  53.6 4.5 %collective-permute-start = (bf16[2,128,512]{2,1,0:T(8,128)(2,1)}, bf16[2,128,512]{2,1,0:T(8,128)(2,1)S(1)}, u32[]{:S(2)}, u32[]{:S(2)}) collective-permute-start(bf16[2,128,512]{2,1,0:T(8,128)(2,1)} %get-tuple-element.10), channel_id=1, source_target_pairs={{0,4},{1,5},{2,6},{3,7},{8,12},{9,13},{10,14},{11,15},{16,20},{17,... | collective-permute-start | bytes 786440 | tf_op jit(solution)/shard_map/ppermute | solution.py:241
  58.1 0.0 copy-done
  58.1 0.6 constant_dynamic-slice_fusion.gain_ref
  58.7 0.4 all-to-all-done.q_ref
  59.1 0.0 copy-start.1
  59.1 5.3 %collective-permute-done.state_ref = bf16[2,128,512]{2,1,0:T(8,128)(2,1)S(1)} collective-permute-done((bf16[2,128,512]{2,1,0:T(8,128)(2,1)}, bf16[2,128,512]{2,1,0:T(8,128)(2,1)S(1)}, u32[]{:S(2)}, u32[]{:S(2)}) %collective-permute-start) | collective-permute-done | bytes 262176 | tf_op jit(solution)/shard_map/ppermute | solution.py:241
  64.5 0.0 copy-done.1
  64.5 0.0 copy-start.2
  64.5 0.7 copy-done.2
  65.2 17.6 %readout.1 = bf16[16,256,128]{2,1,0:T(8,128)(2,1)} custom-call(bf16[16,256,128]{2,1,0:T(8,128)(2,1)} %copy-done.1, bf16[16,528,128]{2,1,0:T(8,128)(2,1)} %all_to_all.15.kv_ref, bf16[2,128,512]{2,1,0:T(8,128)(2,1)} %copy-done.2, f32[2,128]{1,0:T(2,128)} %constant_dynamic-slice_fusion.gain_ref), custom_call_target="tpu_custom_call" | custom-call | flops 2147483648 | bytes 4325376 | tf_op jit(solution)/shard_map/readout/pallas_call | solution.py:219
  82.8 26.6 %all_to_all.16 = bf16[16,256,128]{2,1,0:T(8,128)(2,1)S(1)} all-to-all(bf16[16,256,128]{2,1,0:T(8,128)(2,1)} %readout.1), channel_id=1, replica_groups=mesh['mem'=4,'hi'=2,'lo'=4] {'lo','mem'}, dimensions={0} | all-to-all | bytes 2097152 | tf_op jit(solution)/shard_map/all_to_all | solution.py:281
  109.4 1.6 %copy.10 = bf16[32,128,128]{2,0,1:T(8,128)(2,1)} copy(bf16[32,128,128]{2,1,0:T(8,128)(2,1)S(1)} %bitcast.20) | data formatting | bytes 2097152 | tf_op jit(solution)/shard_map/reshape | solution.py:282
Async XLA Ops:
  0.0 58.1 %copy-start = (f32[4096]{0:T(1024)S(1)}, f32[4096]{0:T(1024)}, u32[]{:S(2)}) copy-start(f32[4096]{0:T(1024)} %param.13) | copy-start | bytes 49156
  39.3 19.8 %all-to-all-start = ((bf16[16,256,128]{2,1,0:T(8,128)(2,1)}), bf16[16,256,128]{2,1,0:T(8,128)(2,1)S(1)}, u32[]{:S(2)}, u32[]{:S(2)}) async-start(bf16[16,256,128]{2,1,0:T(8,128)(2,1)} %get-tuple-element.8), calls=%async_computation | async-start | bytes 2097152 | tf_op jit(solution)/shard_map/all_to_all | solution.py:275
  53.6 10.9 %collective-permute-start = (bf16[2,128,512]{2,1,0:T(8,128)(2,1)}, bf16[2,128,512]{2,1,0:T(8,128)(2,1)S(1)}, u32[]{:S(2)}, u32[]{:S(2)}) collective-permute-start(bf16[2,128,512]{2,1,0:T(8,128)(2,1)} %get-tuple-element.10), channel_id=1, source_target_pairs={{0,4},{1,5},{2,6},{3,7},{8,12},{9,13},{10,14},{11,15},{16,20},{17,... | collective-permute-start | bytes 786440 | tf_op jit(solution)/shard_map/ppermute | solution.py:241
  59.1 5.3 %copy-start.1 = (bf16[16,256,128]{2,1,0:T(8,128)(2,1)}, bf16[16,256,128]{2,1,0:T(8,128)(2,1)S(1)}, u32[]{:S(2)}) copy-start(bf16[16,256,128]{2,1,0:T(8,128)(2,1)S(1)} %all-to-all-done.q_ref) | copy-start | bytes 3145732
  64.5 0.7 copy-start.2

commit v2 on v1

v2 whole, which is shorter than its diff:
```python
import functools
import math

import jax
import jax.numpy as jnp
from jax import lax
from jax.experimental import pallas as pl
from jax.experimental.pallas import tpu as pltpu
from jax.sharding import Mesh
from jax.sharding import PartitionSpec as P

F32 = jnp.float32
BF16 = jnp.bfloat16
META = 16
ROWS = 8


def dot(a, b, dims=((1,), (0,))):
    return lax.dot_general(a, b, (dims, ((), ())), preferred_element_type=F32)


def split_heads(src, out, scr, hl, base, turned):
    td, hb, hd = src.shape
    scr[...] = src[...].astype(F32).reshape(td * hb, hd)
    for j in range(hb):
        start = base + (j % hl) * td
        rows = scr[pl.ds(j, td, stride=hb), :].astype(BF16)
        out[j // hl, start : start + td, :] = rows.T if turned else rows


def pack_kv_kernel(hl, k_ref, v_ref, ld_ref, rt_ref, wt_ref, out, scr_k, scr_v, ld_scr):
    i = pl.program_id(0)
    td, hb, _ = k_ref.shape

    @pl.when(i == 0)
    def _():
        ld_scr[...] = ld_ref[...].astype(F32)

    split_heads(k_ref, out, scr_k, hl, 0, False)
    split_heads(v_ref, out, scr_v, hl, hl * td, True)
    w = wt_ref[...]
    hi = w.astype(BF16).astype(F32)
    mid = (w - hi).astype(BF16).astype(F32)
    low = (w - hi) - mid
    table = jnp.concatenate([rt_ref[...].astype(F32), hi, mid, low], axis=0)
    here = ld_scr[pl.ds(pl.multiple_of(i * hb, hb), hb), :]
    for dd in range(hb // hl):
        own = (here if dd == 0 else pltpu.roll(here, hb - dd * hl, 0))[: META - ROWS]
        out[dd, 2 * hl * td :, :] = jnp.concatenate([table, own], axis=0).astype(BF16)


def pack_q_kernel(hl, q_ref, out, scr):
    split_heads(q_ref, out, scr, hl, 0, True)


def pack_kv(keys, values, ld_t, routes_t, weight_t, g, hl):
    td, heads, hd = keys.shape
    hb = math.gcd(heads, 16)
    rows = 2 * hl * td + META
    whole = lambda a: pl.BlockSpec(a.shape, lambda i: (0,) * a.ndim)
    block = pl.BlockSpec((td, hb, hd), lambda i: (0, i, 0))
    return pl.pallas_call(
        functools.partial(pack_kv_kernel, hl),
        grid=(heads // hb,),
        in_specs=[block, block, whole(ld_t), whole(routes_t), whole(weight_t)],
        out_specs=pl.BlockSpec((hb // hl, rows, hd), lambda i: (i, 0, 0)),
        out_shape=jax.ShapeDtypeStruct((g, rows, hd), BF16),
        scratch_shapes=[pltpu.VMEM((td * hb, hd), F32)] * 2 + [pltpu.VMEM((heads, td), F32)],
        name="pack_kv",
    )(keys, values, ld_t, routes_t, weight_t)


def pack_q(queries, g, hl):
    td, heads, hd = queries.shape
    hb = math.gcd(heads, 16)
    return pl.pallas_call(
        functools.partial(pack_q_kernel, hl),
        grid=(heads // hb,),
        in_specs=[pl.BlockSpec((td, hb, hd), lambda i: (0, i, 0))],
        out_specs=pl.BlockSpec((hb // hl, hl * td, hd), lambda i: (i, 0, 0)),
        out_shape=jax.ShapeDtypeStruct((g, hl * td, hd), BF16),
        scratch_shapes=[pltpu.VMEM((td * hb, hd), F32)],
        name="pack_q",
    )(queries)


def meta_rows(meta_ref, s, hl, memories):
    meta = meta_ref[s].astype(F32)
    td = meta.shape[1]
    row = lax.broadcasted_iota(jnp.int32, (ROWS, td), 0)
    memory = lax.rem(row, memories).astype(F32)
    first = meta[0:1] == memory
    second = meta[1:2] == memory
    rate = jnp.broadcast_to(meta[8:9], (ROWS, td))
    for h in range(1, hl):
        rate = jnp.where(row >= h * memories, meta[8 + h : 9 + h], rate)
    member = first | second
    return meta, first, second, member, jnp.where(member, rate, 0.0)


def running_sums(meta_ref, a_scr, cs_scr, g, hl, memories):
    td = a_scr.shape[1]
    for s in range(g):
        a_scr[s * ROWS : (s + 1) * ROWS, :] = meta_rows(meta_ref, s, hl, memories)[4]
    t0 = lax.broadcasted_iota(jnp.int32, (td, 2 * td), 0)
    t1 = lax.broadcasted_iota(jnp.int32, (td, 2 * td), 1)
    upper = jnp.where(t0 <= t1, 1.0, 0.0).astype(BF16)
    cs_scr[...] = dot(a_scr[...].astype(BF16), upper)


def state_kernel(
    g, hl, memories, td, meta_ref, kv_ref, state_ref, total_ref, a_scr, cs_scr, dec_scr, acc_scr
):
    i = pl.program_id(0)
    step = kv_ref.shape[0]
    hd = kv_ref.shape[2]

    @pl.when(i == 0)
    def _():
        running_sums(meta_ref, a_scr, cs_scr, g, hl, memories)
        after = jnp.zeros((ROWS, td), F32)
        for s in reversed(range(g)):
            member = meta_rows(meta_ref, s, hl, memories)[3]
            rows = slice(s * ROWS, (s + 1) * ROWS)
            running, total = cs_scr[rows, :td], cs_scr[rows, td:]
            dec_scr[s // step, :, s % step * td : (s % step + 1) * td] = jnp.where(
                member, jnp.exp(total - running + after), 0.0
            )
            after = after + total
        total_ref[...] = jnp.exp(after)
        acc_scr[...] = jnp.zeros_like(acc_scr)

    decay = dec_scr[i]
    for h in range(hl):
        key = jnp.concatenate([kv_ref[n, h * td : (h + 1) * td, :] for n in range(step)], axis=0)
        value = jnp.concatenate(
            [kv_ref[n, (hl + h) * td : (hl + h + 1) * td, :] for n in range(step)], axis=1
        ).astype(F32)
        for m in range(memories):
            j = h * memories + m
            acc_scr[h, m * hd : (m + 1) * hd, :] += dot((value * decay[j : j + 1, :]).astype(BF16), key)

    @pl.when(i == pl.num_programs(0) - 1)
    def _():
        state_ref[...] = acc_scr[...].astype(BF16)


def chunk_specs(kv, hl, td, step):
    g, rows, hd = kv.shape
    meta = pl.BlockSpec((g, META, hd), lambda i: (0, 2 * hl * td // META, 0))
    tokens = pl.BlockSpec((step, 2 * hl * td, hd), lambda i: (i, 0, 0))
    return [meta, tokens]


def local_state(kv, hl, memories, td):
    g, rows, hd = kv.shape
    step = math.gcd(g, 8)
    return pl.pallas_call(
        functools.partial(state_kernel, g, hl, memories, td),
        grid=(g // step,),
        in_specs=chunk_specs(kv, hl, td, step),
        out_specs=[
            pl.BlockSpec((hl, memories * hd, hd), lambda i: (0, 0, 0)),
            pl.BlockSpec((ROWS, td), lambda i: (0, 0)),
        ],
        out_shape=[
            jax.ShapeDtypeStruct((hl, memories * hd, hd), BF16),
            jax.ShapeDtypeStruct((ROWS, td), F32),
        ],
        scratch_shapes=[
            pltpu.VMEM((g * ROWS, td), F32),
            pltpu.VMEM((g * ROWS, 2 * td), F32),
            pltpu.VMEM((g // step, ROWS, step * td), F32),
            pltpu.VMEM((hl, memories * hd, hd), F32),
        ],
        cost_estimate=pl.CostEstimate(
            flops=2 * g * td * hl * memories * hd * hd, bytes_accessed=kv.size * 2, transcendentals=0
        ),
        name="local_state",
    )(kv, kv)


def chunk_kernel(
    g, hl, memories, td, meta_ref, kv_ref, lhs_ref, fac_ref, a_scr, cs_scr, col_scr, own_scr, st_scr
):
    i = pl.program_id(0)
    step = kv_ref.shape[0]
    hd = kv_ref.shape[2]
    scale = hd ** (-0.5)

    @pl.when(i == 0)
    def _():
        running_sums(meta_ref, a_scr, cs_scr, g, hl, memories)
        before = jnp.zeros((ROWS, td), F32)
        for s in range(g):
            meta, first, second, member, _ = meta_rows(meta_ref, s, hl, memories)
            rows = slice(s * ROWS, (s + 1) * ROWS)
            running, total = cs_scr[rows, :td], cs_scr[rows, td:]
            half = 0.5 * total
            weight = [meta[2 + n : 3 + n] + (meta[4 + n : 5 + n] + meta[6 + n : 7 + n]) for n in range(2)]
            col_scr[s] = jnp.where(member, jnp.exp(half - running), 0.0)
            own_scr[s] = jnp.exp(half)
            fac_ref[s, 0:ROWS, :] = jnp.exp(running - half) * scale
            fac_ref[s, ROWS : 2 * ROWS, :] = jnp.where(first, weight[0], 0.0) + jnp.where(
                second, weight[1], 0.0
            )
            fac_ref[s, 2 * ROWS :, :] = jnp.exp(before + half)
            before = before + total
        st_scr[...] = jnp.zeros_like(st_scr)

    for n in range(step):
        decay = col_scr[i * step + n]
        own = own_scr[i * step + n]
        for h in range(hl):
            key = kv_ref[n, h * td : (h + 1) * td, :]
            value = kv_ref[n, (hl + h) * td : (hl + h + 1) * td, :].astype(F32)
            for m in range(memories):
                j = h * memories + m
                rows = slice(m * hd, (m + 1) * hd)
                scaled = (value * decay[j : j + 1, :]).astype(BF16)
                lhs_ref[n, h, rows, :td] = scaled
                grown = dot(scaled, key)
                state = st_scr[h, rows, :] * own[j : j + 1, :]
                lhs_ref[n, h, rows, td:] = state.astype(BF16)
                st_scr[h, rows, :] = (state + grown) * own[j : j + 1, :]


def chunk_states(kv, hl, memories, td):
    g, rows, hd = kv.shape
    step = math.gcd(g, 8)
    return pl.pallas_call(
        functools.partial(chunk_kernel, g, hl, memories, td),
        grid=(g // step,),
        in_specs=chunk_specs(kv, hl, td, step),
        out_specs=[
            pl.BlockSpec((step, hl, memories * hd, td + hd), lambda i: (i, 0, 0, 0)),
            pl.BlockSpec((g, 3 * ROWS, td), lambda i: (0, 0, 0)),
        ],
        out_shape=[
            jax.ShapeDtypeStruct((g, hl, memories * hd, td + hd), BF16),
            jax.ShapeDtypeStruct((g, 3 * ROWS, td), F32),
        ],
        scratch_shapes=[
            pltpu.VMEM((g * ROWS, td), F32),
            pltpu.VMEM((g * ROWS, 2 * td), F32),
            pltpu.VMEM((g, ROWS, td), F32),
            pltpu.VMEM((g, ROWS, td), F32),
            pltpu.VMEM((hl, memories * hd, hd), F32),
        ],
        cost_estimate=pl.CostEstimate(
            flops=2 * g * td * hl * memories * hd * hd, bytes_accessed=kv.size * 10, transcendentals=0
        ),
        name="chunk_states",
    )(kv, kv)


def readout_kernel(
    hl, memories, td, q_ref, k_ref, lhs_ref, fac_ref, state_ref, gain_ref, out_ref, st_scr, gain_scr, acc_scr
):
    hd = q_ref.shape[2]

    @pl.when(pl.program_id(0) == 0)
    def _():
        st_scr[...] = state_ref[...].astype(F32)
        for h in range(hl):
            gain_scr[h] = jnp.broadcast_to(gain_ref[h : h + 1, :], (td, hd)).T

    causal = lax.broadcasted_iota(jnp.int32, (td, td), 0) <= lax.broadcasted_iota(jnp.int32, (td, td), 1)
    units = [(c, h) for c in range(q_ref.shape[0]) for h in range(hl)]
    right = []
    for c, h in units:
        query = q_ref[c, h * td : (h + 1) * td, :]
        key = k_ref[c, h * td : (h + 1) * td, :]
        scores = jnp.where(causal, dot(key, query), 0.0).astype(BF16)
        right.append(jnp.concatenate([scores, query], axis=0))
    for u, (c, h) in enumerate(units):
        for m in range(memories):
            j = 2 * ROWS + h * memories + m
            rows = slice(m * hd, (m + 1) * hd)
            state = lhs_ref[c, h, rows, td:].astype(F32) + st_scr[h, rows, :] * fac_ref[c, j : j + 1, :]
            left = jnp.concatenate([lhs_ref[c, h, rows, :td], state.astype(BF16)], axis=1)
            acc_scr[u, rows, :] = dot(left, right[u])
    for u, (c, h) in enumerate(units):
        mixed = jnp.zeros((hd, td), F32)
        for m in range(memories):
            j = h * memories + m
            read = acc_scr[u, m * hd : (m + 1) * hd, :] * fac_ref[c, j : j + 1, :]
            mean = jnp.sum(read * read, axis=0, keepdims=True) * (1.0 / hd)
            mixed = mixed + read * (lax.rsqrt(mean + 1e-06) * fac_ref[c, ROWS + j : ROWS + j + 1, :])
        out_ref[c, h * td : (h + 1) * td, :] = (mixed * gain_scr[h]).astype(BF16).T


def readout(q, kv, lhs, factors, state, gain, hl, memories, td):
    g, rows, hd = q.shape
    step = math.gcd(g, 8)
    tokens = pl.BlockSpec((step, hl * td, hd), lambda i: (i, 0, 0))
    return pl.pallas_call(
        functools.partial(readout_kernel, hl, memories, td),
        grid=(g // step,),
        in_specs=[
            tokens,
            tokens,
            pl.BlockSpec((step,) + lhs.shape[1:], lambda i: (i, 0, 0, 0)),
            pl.BlockSpec((step,) + factors.shape[1:], lambda i: (i, 0, 0)),
            pl.BlockSpec(state.shape, lambda i: (0, 0, 0)),
            pl.BlockSpec(gain.shape, lambda i: (0, 0)),
        ],
        out_specs=tokens,
        out_shape=jax.ShapeDtypeStruct(q.shape, BF16),
        scratch_shapes=[
            pltpu.VMEM(state.shape, F32),
            pltpu.VMEM((hl, hd, td), F32),
            pltpu.VMEM((step * hl, memories * hd, td), F32),
        ],
        cost_estimate=pl.CostEstimate(
            flops=8 * g * td * hl * memories * hd * hd, bytes_accessed=kv.size * 10, transcendentals=0
        ),
        name="readout",
    )(q, kv, lhs, factors, state, gain)


def entering_state(state, total, groups, hl, memories):
    if groups == 1:
        return jnp.zeros_like(state)
    state = lax.ppermute(state, "hi", [(i, i + 1) for i in range(groups - 1)])
    if groups == 2:
        return state
    factor = lax.ppermute(total[:, :1], "hi", [(i, i + 1) for i in range(groups - 1)])

    def spread(f):
        wide = jnp.broadcast_to(f.reshape(hl, memories, 1), (hl, memories, state.shape[2]))
        return wide.reshape(hl, state.shape[1], 1)

    held = state.astype(F32)
    step = 1
    while step < groups - 1:
        pairs = [(i, i + step) for i in range(groups - step)]
        earlier = lax.ppermute(held.astype(BF16), "hi", pairs).astype(F32)
        earlier_factor = lax.ppermute(factor, "hi", pairs)
        held = held + spread(factor) * earlier
        factor = factor * earlier_factor
        step *= 2
    return held.astype(BF16)


def shards(queries, keys, values, log_decay, routes, route_weight, gain):
    td, heads, hd = queries.shape[1:]
    memories = lax.axis_size("mem")
    lo = lax.axis_size("lo")
    groups = lax.axis_size("hi")
    g = memories * lo
    hl = heads // g
    axes = ("lo", "mem")
    kv_send = pack_kv(
        keys[0], values[0], log_decay[0].T, routes[0].T, route_weight[0].T, g, hl
    )
    q_send = pack_q(queries[0], g, hl)
    kv = lax.all_to_all(kv_send, axes, split_axis=0, concat_axis=0, tiled=True)
    q = lax.all_to_all(q_send, axes, split_axis=0, concat_axis=0, tiled=True)
    state, total = local_state(kv, hl, memories, td)
    entering = entering_state(state, total, groups, hl, memories)
    place = lax.axis_index("lo") * memories + lax.axis_index("mem")
    own_gain = lax.dynamic_slice_in_dim(gain.reshape(heads, hd), place * hl, hl, 0)
    lhs, factors = chunk_states(kv, hl, memories, td)
    out = readout(q, kv, lhs, factors, entering, own_gain, hl, memories, td)
    back = lax.all_to_all(out, axes, split_axis=0, concat_axis=0, tiled=True)
    return back.reshape(heads, td, hd).transpose(1, 0, 2)[None]


def solution(mesh):
    memories, blocks = mesh.shape["mem"], mesh.shape["ctx"]
    def call(queries, keys, values, log_decay, routes, route_weight, gain):
        heads = queries.shape[2]
        lo = max(
            s
            for s in range(1, max(1, blocks // 2) + 1)
            if blocks % s == 0 and heads % (memories * s) == 0
        )
        split = Mesh(mesh.devices.reshape(memories, blocks // lo, lo), ("mem", "hi", "lo"))
        tokens = P(("hi", "lo"), "mem")
        return jax.shard_map(
            shards,
            mesh=split,
            in_specs=(tokens,) * 6 + (P(),),
            out_specs=tokens,
            check_vma=False,
        )(queries, keys, values, log_decay, routes, route_weight, gain)

    return call
```

time: 112 us -> 95.6 us (0.85)
  blocking collectives: 61.1 us -> 23 us
  waiting for transfers between devices: 5.75 us -> 31.4 us
  Pallas kernels: 33.1 us -> 23.3 us
  starting transfers between devices: 8.15 us -> 14.5 us
    all_to_all x1 -> x0, blocking collectives: 34.5 us -> none  [shards(): kv = lax.all_to_all(kv_send, axes, split_axis=0, concat_axis=0, tiled=True)]
    all_to_all x0 -> x1, waiting for transfers between devices: none -> 27.9 us  [shards(): kv = lax.all_to_all(kv_send, axes, split_axis=0, concat_axis=0, tiled=True)]
    pallas_call x3 -> x5, Pallas kernels: 33.1 us -> 23.3 us  [the longest x1 7.24 us: readout(): pl.pallas_call(functools.partial(readout_kernel, hl, memories, td), grid=...]
    all_to_all x0 -> x1, starting transfers between devices: none -> 6.32 us  [shards(): kv = lax.all_to_all(kv_send, axes, split_axis=0, concat_axis=0, tiled=True)]
    all_to_all x1, blocking collectives: 26.6 us -> 23 us  [shards(): back = lax.all_to_all(out, axes, split_axis=0, concat_axis=0, tiled=True)]
    ppermute x1, waiting for transfers between devices: 5.32 us -> 1.97 us  [entering_state(): state = lax.ppermute(state, 'hi', [(i, i + 1) for i in range(groups - 1)])]
    all_to_all x1, waiting for transfers between devices: 0.43 us -> 1.56 us  [shards(): q = lax.all_to_all(q_send, axes, split_axis=0, concat_axis=0, tiled=True)]
  transfers between devices with their start and end apart: 2 -> 3, of which waited for: 2 -> 3; matrix products, arithmetic and copies ran while one was open for 1% -> 1% of each run, Pallas kernels for 10% -> 13%
where the time goes in v2:
time: 95.6 us; the launch traced here: 95.2 us
  waiting for transfers between devices  31.4 us (33%)
  Pallas kernels  23.3 us (24%)
  blocking collectives  23 us (24%)
  starting transfers between devices  14.5 us (15%)
  local copies, waits for them, and re-layouts  2.96 us (3%)
    all_to_all x1, waiting for transfers between devices, shards(): kv = lax.all_to_all(kv_send, axes, split_axis=0, concat_axis=0, tiled=True)  27.9 us
    all_to_all x1, blocking collectives, shards(): back = lax.all_to_all(out, axes, split_axis=0, concat_axis=0, tiled=True)  23 us
    pallas_call x1, Pallas kernels, readout(): pl.pallas_call(functools.partial(readout_kernel, hl, memories, td), grid=...  7.24 us
    all_to_all x1, starting transfers between devices, shards(): kv = lax.all_to_all(kv_send, axes, split_axis=0, concat_axis=0, tiled=True)  6.32 us
    pallas_call x1, Pallas kernels, chunk_states(): pl.pallas_call(functools.partial(chunk_kernel, g, hl, memories, td), grid...  5.88 us
    ppermute x1, starting transfers between devices, entering_state(): state = lax.ppermute(state, 'hi', [(i, i + 1) for i in range(groups - 1)])  4.5 us
    pallas_call x1, Pallas kernels, pack_kv(): pl.pallas_call(functools.partial(pack_kv_kernel, hl), grid=(heads // hb,)...  3.82 us
    all_to_all x1, starting transfers between devices, shards(): q = lax.all_to_all(q_send, axes, split_axis=0, concat_axis=0, tiled=True)  3.69 us
  transfers between devices with their start and end apart: 3, of which 3 were waited for; matrix products, arithmetic and copies ran while one was open for 1% of the time, Pallas kernels for 13%

profile of v2, /device:TPU:0, one launch (start us, length us, event | category | flops | bytes accessed | tf_op | source)
XLA Modules:
  0.0 95.2 jit_solution(15371384217005873199)
XLA Ops:
  0.0 0.0 copy-start
  0.0 3.8 %pack_kv.1 = bf16[16,528,128]{2,1,0:T(8,128)(2,1)} custom-call(bf16[128,32,128]{2,1,0:T(8,128)(2,1)} %bitcast.22, bf16[128,32,128]{2,1,0:T(8,128)(2,1)} %bitcast.23, bf16[32,128]{1,0:T(8,128)(2,1)} %bitcast.24, s32[2,128]{1,0:T(2,128)} %bitcast.25, f32[2,128]{1,0:T(2,128)} %bitcast.26), custom_call_target="tpu_custom_call" | custom-call | tf_op jit(solution)/shard_map/pack_kv/pallas_call | solution.py:62
  3.8 6.3 %all-to-all-start.1 = ((bf16[16,528,128]{2,1,0:T(8,128)(2,1)}), bf16[16,528,128]{2,1,0:T(8,128)(2,1)S(1)}, u32[]{:S(2)}, u32[]{:S(2)}) async-start(bf16[16,528,128]{2,1,0:T(8,128)(2,1)} %pack_kv.1), calls=%async_computation.1 | async-start | bytes 4325376 | tf_op jit(solution)/shard_map/all_to_all | solution.py:358
  10.2 2.7 %pack_q.1 = bf16[16,256,128]{2,1,0:T(8,128)(2,1)} custom-call(bf16[128,32,128]{2,1,0:T(8,128)(2,1)} %bitcast.21), custom_call_target="tpu_custom_call" | custom-call | tf_op jit(solution)/shard_map/pack_q/pallas_call | solution.py:76
  12.9 27.9 %all-to-all-done.1.meta_ref.kv_ref.k_ref = bf16[16,528,128]{2,1,0:T(8,128)(2,1)S(1)} async-done(((bf16[16,528,128]{2,1,0:T(8,128)(2,1)}), bf16[16,528,128]{2,1,0:T(8,128)(2,1)S(1)}, u32[]{:S(2)}, u32[]{:S(2)}) %all-to-all-start.1) | async-done | bytes 2162720 | tf_op jit(solution)/shard_map/all_to_all | solution.py:358
  40.8 0.0 copy-start.1
  40.8 3.7 %all-to-all-start = ((bf16[16,256,128]{2,1,0:T(8,128)(2,1)}), bf16[16,256,128]{2,1,0:T(8,128)(2,1)S(1)}, u32[]{:S(2)}, u32[]{:S(2)}) async-start(bf16[16,256,128]{2,1,0:T(8,128)(2,1)} %pack_q.1), calls=%async_computation | async-start | bytes 2097152 | tf_op jit(solution)/shard_map/all_to_all | solution.py:359
  44.5 0.0 copy-done.1
  44.5 3.6 %local_state.1 = (bf16[2,512,128]{2,1,0:T(8,128)(2,1)}, f32[8,128]{1,0:T(8,128)}) custom-call(bf16[16,528,128]{2,1,0:T(8,128)(2,1)} %copy-done.1, bf16[16,528,128]{2,1,0:T(8,128)(2,1)} %copy-done.1), custom_call_target="tpu_custom_call" | custom-call | flops 536870912 | bytes 2162688 | tf_op jit(solution)/shard_map/local_state/pallas_call | solution.py:158
  48.1 4.5 %collective-permute-start = (bf16[2,512,128]{2,1,0:T(8,128)(2,1)}, bf16[2,512,128]{2,1,0:T(8,128)(2,1)S(1)}, u32[]{:S(2)}, u32[]{:S(2)}) collective-permute-start(bf16[2,512,128]{2,1,0:T(8,128)(2,1)} %get-tuple-element.10), channel_id=1, source_target_pairs={{0,4},{1,5},{2,6},{3,7},{8,12},{9,13},{10,14},{11,15},{16,20},{17,... | collective-permute-start | bytes 786440 | tf_op jit(solution)/shard_map/ppermute | solution.py:325
  52.6 0.0 copy-done
  52.6 0.6 constant_dynamic-slice_fusion.gain_ref
  53.2 5.9 %chunk_states.1 = (bf16[16,2,512,256]{3,2,1,0:T(8,128)(2,1)}, f32[16,24,128]{2,1,0:T(8,128)}) custom-call(bf16[16,528,128]{2,1,0:T(8,128)(2,1)} %copy-done.1, bf16[16,528,128]{2,1,0:T(8,128)(2,1)} %copy-done.1), custom_call_target="tpu_custom_call" | custom-call | flops 536870912 | bytes 10813440 | tf_op jit(solution)/shard_map/chunk_states/pallas_call | solution.py:231
  59.1 1.6 %all-to-all-done.q_ref = bf16[16,256,128]{2,1,0:T(8,128)(2,1)S(1)} async-done(((bf16[16,256,128]{2,1,0:T(8,128)(2,1)}), bf16[16,256,128]{2,1,0:T(8,128)(2,1)S(1)}, u32[]{:S(2)}, u32[]{:S(2)}) %all-to-all-start) | async-done | bytes 1048608 | tf_op jit(solution)/shard_map/all_to_all | solution.py:359
  60.6 0.0 copy-start.2
  60.6 2.0 %collective-permute-done.state_ref = bf16[2,512,128]{2,1,0:T(8,128)(2,1)S(1)} collective-permute-done((bf16[2,512,128]{2,1,0:T(8,128)(2,1)}, bf16[2,512,128]{2,1,0:T(8,128)(2,1)S(1)}, u32[]{:S(2)}, u32[]{:S(2)}) %collective-permute-start) | collective-permute-done | bytes 262176 | tf_op jit(solution)/shard_map/ppermute | solution.py:325
  62.6 0.0 copy-start.3
  62.6 0.0 copy-done.2
  62.6 0.7 copy-done.3
  63.3 7.2 %readout.1 = bf16[16,256,128]{2,1,0:T(8,128)(2,1)} custom-call(bf16[16,256,128]{2,1,0:T(8,128)(2,1)} %copy-done.2, bf16[16,528,128]{2,1,0:T(8,128)(2,1)} %copy-done.1, bf16[16,2,512,256]{3,2,1,0:T(8,128)(2,1)} %get-tuple-element.8.lhs_ref, f32[16,24,128]{2,1,0:T(8,128)} %get-tuple-element.9.fac_ref, bf16[2,512,128]{2,1,0:T(8,128)(2,1)} %copy-done.3, ...), custom_call_target="tpu_custom_call" | custom-call | flops 2147483648 | bytes 10813440 | tf_op jit(solution)/shard_map/readout/pallas_call | solution.py:297
  70.5 23.0 %all_to_all.15 = bf16[16,256,128]{2,1,0:T(8,128)(2,1)S(1)} all-to-all(bf16[16,256,128]{2,1,0:T(8,128)(2,1)} %readout.1), channel_id=1, replica_groups=mesh['mem'=4,'hi'=2,'lo'=4] {'lo','mem'}, dimensions={0} | all-to-all | bytes 2097152 | tf_op jit(solution)/shard_map/all_to_all | solution.py:366
  93.5 1.6 %copy.10 = bf16[32,128,128]{2,0,1:T(8,128)(2,1)} copy(bf16[32,128,128]{2,1,0:T(8,128)(2,1)S(1)} %bitcast.20) | data formatting | bytes 2097152 | tf_op jit(solution)/shard_map/reshape | solution.py:367
Async XLA Ops:
  0.0 52.6 %copy-start = (f32[4096]{0:T(1024)S(1)}, f32[4096]{0:T(1024)}, u32[]{:S(2)}) copy-start(f32[4096]{0:T(1024)} %param.13) | copy-start | bytes 49156
  3.8 36.9 %all-to-all-start.1 = ((bf16[16,528,128]{2,1,0:T(8,128)(2,1)}), bf16[16,528,128]{2,1,0:T(8,128)(2,1)S(1)}, u32[]{:S(2)}, u32[]{:S(2)}) async-start(bf16[16,528,128]{2,1,0:T(8,128)(2,1)} %pack_kv.1), calls=%async_computation.1 | async-start | bytes 4325376 | tf_op jit(solution)/shard_map/all_to_all | solution.py:358
  40.8 3.7 %copy-start.1 = (bf16[16,528,128]{2,1,0:T(8,128)(2,1)}, bf16[16,528,128]{2,1,0:T(8,128)(2,1)S(1)}, u32[]{:S(2)}) copy-start(bf16[16,528,128]{2,1,0:T(8,128)(2,1)S(1)} %all-to-all-done.1.meta_ref.kv_ref.k_ref) | copy-start | bytes 6488068
  40.8 19.9 %all-to-all-start = ((bf16[16,256,128]{2,1,0:T(8,128)(2,1)}), bf16[16,256,128]{2,1,0:T(8,128)(2,1)S(1)}, u32[]{:S(2)}, u32[]{:S(2)}) async-start(bf16[16,256,128]{2,1,0:T(8,128)(2,1)} %pack_q.1), calls=%async_computation | async-start | bytes 2097152 | tf_op jit(solution)/shard_map/all_to_all | solution.py:359
  48.1 14.5 %collective-permute-start = (bf16[2,512,128]{2,1,0:T(8,128)(2,1)}, bf16[2,512,128]{2,1,0:T(8,128)(2,1)S(1)}, u32[]{:S(2)}, u32[]{:S(2)}) collective-permute-start(bf16[2,512,128]{2,1,0:T(8,128)(2,1)} %get-tuple-element.10), channel_id=1, source_target_pairs={{0,4},{1,5},{2,6},{3,7},{8,12},{9,13},{10,14},{11,15},{16,20},{17,... | collective-permute-start | bytes 786440 | tf_op jit(solution)/shard_map/ppermute | solution.py:325
  60.6 2.0 %copy-start.2 = (bf16[16,256,128]{2,1,0:T(8,128)(2,1)}, bf16[16,256,128]{2,1,0:T(8,128)(2,1)S(1)}, u32[]{:S(2)}) copy-start(bf16[16,256,128]{2,1,0:T(8,128)(2,1)S(1)} %all-to-all-done.q_ref) | copy-start | bytes 3145732
  62.6 0.7 copy-start.3

commit v3 on v2

--- a/solution.py
+++ b/solution.py
@@ -12,6 +12,7 @@
 F32 = jnp.float32
 BF16 = jnp.bfloat16
 META = 16
+PARAMS = pltpu.CompilerParams(vmem_limit_bytes=50 << 20)
 ROWS = 8
 
 
@@ -19,25 +20,26 @@
     return lax.dot_general(a, b, (dims, ((), ())), preferred_element_type=F32)
 
 
-def split_heads(src, out, scr, hl, base, turned):
+def split_heads(src, place, scr, hl, base, turned):
     td, hb, hd = src.shape
     scr[...] = src[...].astype(F32).reshape(td * hb, hd)
     for j in range(hb):
         start = base + (j % hl) * td
         rows = scr[pl.ds(j, td, stride=hb), :].astype(BF16)
-        out[j // hl, start : start + td, :] = rows.T if turned else rows
-
-
-def pack_kv_kernel(hl, k_ref, v_ref, ld_ref, rt_ref, wt_ref, out, scr_k, scr_v, ld_scr):
+        place(j // hl)[start : start + td, :] = rows.T if turned else rows
+
+
+def pack_kv_kernel(hl, lo, k_ref, v_ref, ld_ref, rt_ref, wt_ref, out, scr_k, scr_v, ld_scr):
     i = pl.program_id(0)
     td, hb, _ = k_ref.shape
+    place = lambda dd: out.at[dd % lo, dd // lo]
 
     @pl.when(i == 0)
     def _():
         ld_scr[...] = ld_ref[...].astype(F32)
 
-    split_heads(k_ref, out, scr_k, hl, 0, False)
-    split_heads(v_ref, out, scr_v, hl, hl * td, True)
+    split_heads(k_ref, place, scr_k, hl, 0, False)
+    split_heads(v_ref, place, scr_v, hl, hl * td, True)
     w = wt_ref[...]
     hi = w.astype(BF16).astype(F32)
     mid = (w - hi).astype(BF16).astype(F32)
@@ -46,25 +48,25 @@
     here = ld_scr[pl.ds(pl.multiple_of(i * hb, hb), hb), :]
     for dd in range(hb // hl):
         own = (here if dd == 0 else pltpu.roll(here, hb - dd * hl, 0))[: META - ROWS]
-        out[dd, 2 * hl * td :, :] = jnp.concatenate([table, own], axis=0).astype(BF16)
+        place(dd)[2 * hl * td :, :] = jnp.concatenate([table, own], axis=0).astype(BF16)
 
 
 def pack_q_kernel(hl, q_ref, out, scr):
-    split_heads(q_ref, out, scr, hl, 0, True)
-
-
-def pack_kv(keys, values, ld_t, routes_t, weight_t, g, hl):
+    split_heads(q_ref, lambda dd: out.at[dd], scr, hl, 0, True)
+
+
+def pack_kv(keys, values, ld_t, routes_t, weight_t, lo, memories, hl):
     td, heads, hd = keys.shape
     hb = math.gcd(heads, 16)
     rows = 2 * hl * td + META
     whole = lambda a: pl.BlockSpec(a.shape, lambda i: (0,) * a.ndim)
     block = pl.BlockSpec((td, hb, hd), lambda i: (0, i, 0))
     return pl.pallas_call(
-        functools.partial(pack_kv_kernel, hl),
+        functools.partial(pack_kv_kernel, hl, lo),
         grid=(heads // hb,),
         in_specs=[block, block, whole(ld_t), whole(routes_t), whole(weight_t)],
-        out_specs=pl.BlockSpec((hb // hl, rows, hd), lambda i: (i, 0, 0)),
-        out_shape=jax.ShapeDtypeStruct((g, rows, hd), BF16),
+        out_specs=pl.BlockSpec((lo, hb // hl // lo, rows, hd), lambda i: (0, i, 0, 0)),
+        out_shape=jax.ShapeDtypeStruct((lo, memories, rows, hd), BF16),
         scratch_shapes=[pltpu.VMEM((td * hb, hd), F32)] * 2 + [pltpu.VMEM((heads, td), F32)],
         name="pack_kv",
     )(keys, values, ld_t, routes_t, weight_t)
@@ -173,6 +175,7 @@
             pltpu.VMEM((g // step, ROWS, step * td), F32),
             pltpu.VMEM((hl, memories * hd, hd), F32),
         ],
+        compiler_params=PARAMS,
         cost_estimate=pl.CostEstimate(
             flops=2 * g * td * hl * memories * hd * hd, bytes_accessed=kv.size * 2, transcendentals=0
         ),
@@ -180,128 +183,142 @@
     )(kv, kv)
 
 
-def chunk_kernel(
-    g, hl, memories, td, meta_ref, kv_ref, lhs_ref, fac_ref, a_scr, cs_scr, col_scr, own_scr, st_scr
-):
-    i = pl.program_id(0)
-    step = kv_ref.shape[0]
+def factor_kernel(g, hl, memories, td, meta_ref, fac_ref, a_scr, cs_scr):
+    scale = meta_ref.shape[2] ** (-0.5)
+    running_sums(meta_ref, a_scr, cs_scr, g, hl, memories)
+    before = jnp.zeros((ROWS, td), F32)
+    for s in range(g):
+        meta, first, second, member, _ = meta_rows(meta_ref, s, hl, memories)
+        rows = slice(s * ROWS, (s + 1) * ROWS)
+        running, total = cs_scr[rows, :td], cs_scr[rows, td:]
+        half = 0.5 * total
+        weight = [meta[2 + n : 3 + n] + (meta[4 + n : 5 + n] + meta[6 + n : 7 + n]) for n in range(2)]
+        fac_ref[s, 0:ROWS, :] = jnp.exp(running - half) * scale
+        fac_ref[s, ROWS : 2 * ROWS, :] = jnp.where(first, weight[0], 0.0) + jnp.where(
+            second, weight[1], 0.0
+        )
+        fac_ref[s, 2 * ROWS : 3 * ROWS, :] = jnp.exp(before + half)
+        fac_ref[s, 3 * ROWS : 4 * ROWS, :] = jnp.where(member, jnp.exp(half - running), 0.0)
+        fac_ref[s, 4 * ROWS :, :] = jnp.exp(half)
+        before = before + total
+
+
+def chunk_factors(kv, hl, memories, td):
+    g, rows, hd = kv.shape
+    return pl.pallas_call(
+        functools.partial(factor_kernel, g, hl, memories, td),
+        grid=(1,),
+        in_specs=chunk_specs(kv, hl, td, 1)[:1],
+        out_specs=pl.BlockSpec((g, 5 * ROWS, td), lambda i: (0, 0, 0)),
+        out_shape=jax.ShapeDtypeStruct((g, 5 * ROWS, td), F32),
+        scratch_shapes=[pltpu.VMEM((g * ROWS, td), F32), pltpu.VMEM((g * ROWS, 2 * td), F32)],
+        compiler_params=PARAMS,
+        cost_estimate=pl.CostEstimate(flops=g * td * td, bytes_accessed=g * td * 200, transcendentals=0),
+        name="chunk_factors",
+    )(kv)
+
+
+def chunk_kernel(hl, memories, td, fac_ref, kv_ref, lhs_ref, st_scr):
     hd = kv_ref.shape[2]
-    scale = hd ** (-0.5)
-
-    @pl.when(i == 0)
+
+    @pl.when(pl.program_id(0) == 0)
     def _():
-        running_sums(meta_ref, a_scr, cs_scr, g, hl, memories)
-        before = jnp.zeros((ROWS, td), F32)
-        for s in range(g):
-            meta, first, second, member, _ = meta_rows(meta_ref, s, hl, memories)
-            rows = slice(s * ROWS, (s + 1) * ROWS)
-            running, total = cs_scr[rows, :td], cs_scr[rows, td:]
-            half = 0.5 * total
-            weight = [meta[2 + n : 3 + n] + (meta[4 + n : 5 + n] + meta[6 + n : 7 + n]) for n in range(2)]
-            col_scr[s] = jnp.where(member, jnp.exp(half - running), 0.0)
-            own_scr[s] = jnp.exp(half)
-            fac_ref[s, 0:ROWS, :] = jnp.exp(running - half) * scale
-            fac_ref[s, ROWS : 2 * ROWS, :] = jnp.where(first, weight[0], 0.0) + jnp.where(
-                second, weight[1], 0.0
-            )
-            fac_ref[s, 2 * ROWS :, :] = jnp.exp(before + half)
-            before = before + total
         st_scr[...] = jnp.zeros_like(st_scr)
 
-    for n in range(step):
-        decay = col_scr[i * step + n]
-        own = own_scr[i * step + n]
+    for n in range(kv_ref.shape[0]):
         for h in range(hl):
             key = kv_ref[n, h * td : (h + 1) * td, :]
             value = kv_ref[n, (hl + h) * td : (hl + h + 1) * td, :].astype(F32)
             for m in range(memories):
                 j = h * memories + m
                 rows = slice(m * hd, (m + 1) * hd)
-                scaled = (value * decay[j : j + 1, :]).astype(BF16)
+                own = fac_ref[n, 4 * ROWS + j : 4 * ROWS + j + 1, :]
+                scaled = (value * fac_ref[n, 3 * ROWS + j : 3 * ROWS + j + 1, :]).astype(BF16)
                 lhs_ref[n, h, rows, :td] = scaled
                 grown = dot(scaled, key)
-                state = st_scr[h, rows, :] * own[j : j + 1, :]
+                state = st_scr[h, rows, :] * own
                 lhs_ref[n, h, rows, td:] = state.astype(BF16)
-                st_scr[h, rows, :] = (state + grown) * own[j : j + 1, :]
-
-
-def chunk_states(kv, hl, memories, td):
+                st_scr[h, rows, :] = (state + grown) * own
+
+
+def chunk_states(kv, factors, hl, memories, td):
     g, rows, hd = kv.shape
     step = math.gcd(g, 8)
     return pl.pallas_call(
-        functools.partial(chunk_kernel, g, hl, memories, td),
+        functools.partial(chunk_kernel, hl, memories, td),
         grid=(g // step,),
-        in_specs=chunk_specs(kv, hl, td, step),
-        out_specs=[
-            pl.BlockSpec((step, hl, memories * hd, td + hd), lambda i: (i, 0, 0, 0)),
-            pl.BlockSpec((g, 3 * ROWS, td), lambda i: (0, 0, 0)),
-        ],
-        out_shape=[
-            jax.ShapeDtypeStruct((g, hl, memories * hd, td + hd), BF16),
-            jax.ShapeDtypeStruct((g, 3 * ROWS, td), F32),
-        ],
-        scratch_shapes=[
-            pltpu.VMEM((g * ROWS, td), F32),
-            pltpu.VMEM((g * ROWS, 2 * td), F32),
-            pltpu.VMEM((g, ROWS, td), F32),
-            pltpu.VMEM((g, ROWS, td), F32),
-            pltpu.VMEM((hl, memories * hd, hd), F32),
-        ],
+        in_specs=[
+            pl.BlockSpec((step,) + factors.shape[1:], lambda i: (i, 0, 0)),
+            chunk_specs(kv, hl, td, step)[1],
+        ],
+        out_specs=pl.BlockSpec((step, hl, memories * hd, td + hd), lambda i: (i, 0, 0, 0)),
+        out_shape=jax.ShapeDtypeStruct((g, hl, memories * hd, td + hd), BF16),
+        scratch_shapes=[pltpu.VMEM((hl, memories * hd, hd), F32)],
+        compiler_params=PARAMS,
         cost_estimate=pl.CostEstimate(
             flops=2 * g * td * hl * memories * hd * hd, bytes_accessed=kv.size * 10, transcendentals=0
         ),
         name="chunk_states",
-    )(kv, kv)
+    )(factors, kv)
 
 
 def readout_kernel(
-    hl, memories, td, q_ref, k_ref, lhs_ref, fac_ref, state_ref, gain_ref, out_ref, st_scr, gain_scr, acc_scr
+    hl, memories, lo, td, q_ref, k_ref, lhs_ref, fac_ref, state_ref, gain_ref, out_ref,
+    st_scr, gain_scr, acc_scr,
 ):
-    hd = q_ref.shape[2]
-
-    @pl.when(pl.program_id(0) == 0)
+    hd = q_ref.shape[3]
+    part = q_ref.shape[0]
+    i = pl.program_id(0)
+
+    @pl.when(i == 0)
     def _():
         st_scr[...] = state_ref[...].astype(F32)
+        place = lax.axis_index("mem") * lo + lax.axis_index("lo")
         for h in range(hl):
-            gain_scr[h] = jnp.broadcast_to(gain_ref[h : h + 1, :], (td, hd)).T
+            own = gain_ref[pl.ds(place * hl + h, 1), :]
+            gain_scr[h] = jnp.broadcast_to(own, (td, hd)).T
 
     causal = lax.broadcasted_iota(jnp.int32, (td, td), 0) <= lax.broadcasted_iota(jnp.int32, (td, td), 1)
-    units = [(c, h) for c in range(q_ref.shape[0]) for h in range(hl)]
+    units = [(a, b, h) for b in range(lo) for a in range(part) for h in range(hl)]
     right = []
-    for c, h in units:
-        query = q_ref[c, h * td : (h + 1) * td, :]
-        key = k_ref[c, h * td : (h + 1) * td, :]
+    for a, b, h in units:
+        query = q_ref[a, b, h * td : (h + 1) * td, :]
+        key = k_ref[b, a, h * td : (h + 1) * td, :]
         scores = jnp.where(causal, dot(key, query), 0.0).astype(BF16)
         right.append(jnp.concatenate([scores, query], axis=0))
-    for u, (c, h) in enumerate(units):
+    for u, (a, b, h) in enumerate(units):
+        s = b * memories + i * part + a
         for m in range(memories):
             j = 2 * ROWS + h * memories + m
             rows = slice(m * hd, (m + 1) * hd)
-            state = lhs_ref[c, h, rows, td:].astype(F32) + st_scr[h, rows, :] * fac_ref[c, j : j + 1, :]
-            left = jnp.concatenate([lhs_ref[c, h, rows, :td], state.astype(BF16)], axis=1)
+            state = lhs_ref[b, a, h, rows, td:].astype(F32) + st_scr[h, rows, :] * fac_ref[s, j : j + 1, :]
+            left = jnp.concatenate([lhs_ref[b, a, h, rows, :td], state.astype(BF16)], axis=1)
             acc_scr[u, rows, :] = dot(left, right[u])
-    for u, (c, h) in enumerate(units):
-        mixed = jnp.zeros((hd, td), F32)
+    for u, (a, b, h) in enumerate(units):
+        s = b * memories + i * part + a
+        mixed = None
         for m in range(memories):
             j = h * memories + m
-            read = acc_scr[u, m * hd : (m + 1) * hd, :] * fac_ref[c, j : j + 1, :]
+            read = acc_scr[u, m * hd : (m + 1) * hd, :] * fac_ref[s, j : j + 1, :]
             mean = jnp.sum(read * read, axis=0, keepdims=True) * (1.0 / hd)
-            mixed = mixed + read * (lax.rsqrt(mean + 1e-06) * fac_ref[c, ROWS + j : ROWS + j + 1, :])
-        out_ref[c, h * td : (h + 1) * td, :] = (mixed * gain_scr[h]).astype(BF16).T
-
-
-def readout(q, kv, lhs, factors, state, gain, hl, memories, td):
-    g, rows, hd = q.shape
-    step = math.gcd(g, 8)
-    tokens = pl.BlockSpec((step, hl * td, hd), lambda i: (i, 0, 0))
-    return pl.pallas_call(
-        functools.partial(readout_kernel, hl, memories, td),
-        grid=(g // step,),
+            term = read * (lax.rsqrt(mean + 1e-06) * fac_ref[s, ROWS + j : ROWS + j + 1, :])
+            mixed = term if mixed is None else mixed + term
+        out_ref[a, b, h * td : (h + 1) * td, :] = (mixed * gain_scr[h]).astype(BF16).T
+
+
+def readout(q, kv, lhs, factors, state, gain, lo, hl, memories, td):
+    g, _, hd = q.shape
+    part = max(1, math.gcd(memories, 8 // math.gcd(lo, 8)))
+    q = q.reshape(memories, lo, hl * td, hd)
+    tokens = pl.BlockSpec((part, lo, hl * td, hd), lambda i: (i, 0, 0, 0))
+    out = pl.pallas_call(
+        functools.partial(readout_kernel, hl, memories, lo, td),
+        grid=(memories // part,),
         in_specs=[
             tokens,
-            tokens,
-            pl.BlockSpec((step,) + lhs.shape[1:], lambda i: (i, 0, 0, 0)),
-            pl.BlockSpec((step,) + factors.shape[1:], lambda i: (i, 0, 0)),
+            pl.BlockSpec((lo, part, hl * td, hd), lambda i: (0, i, 0, 0)),
+            pl.BlockSpec((lo, part) + lhs.shape[1:], lambda i: (0, i, 0, 0, 0)),
+            pl.BlockSpec(factors.shape, lambda i: (0, 0, 0)),
             pl.BlockSpec(state.shape, lambda i: (0, 0, 0)),
             pl.BlockSpec(gain.shape, lambda i: (0, 0)),
         ],
@@ -310,13 +327,22 @@
         scratch_shapes=[
             pltpu.VMEM(state.shape, F32),
             pltpu.VMEM((hl, hd, td), F32),
-            pltpu.VMEM((step * hl, memories * hd, td), F32),
-        ],
+            pltpu.VMEM((part * lo * hl, memories * hd, td), F32),
+        ],
+        compiler_params=PARAMS,
         cost_estimate=pl.CostEstimate(
             flops=8 * g * td * hl * memories * hd * hd, bytes_accessed=kv.size * 10, transcendentals=0
         ),
         name="readout",
-    )(q, kv, lhs, factors, state, gain)
+    )(
+        q,
+        kv.reshape((lo, memories) + kv.shape[1:]),
+        lhs.reshape((lo, memories) + lhs.shape[1:]),
+        factors,
+        state,
+        gain,
+    )
+    return out.reshape(g, hl * td, hd)
 
 
 def entering_state(state, total, groups, hl, memories):
@@ -350,20 +376,18 @@
     groups = lax.axis_size("hi")
     g = memories * lo
     hl = heads // g
-    axes = ("lo", "mem")
     kv_send = pack_kv(
-        keys[0], values[0], log_decay[0].T, routes[0].T, route_weight[0].T, g, hl
-    )
+        keys[0], values[0], log_decay[0].T, routes[0].T, route_weight[0].T, lo, memories, hl
+    ).reshape(g, 2 * hl * td + META, hd)
     q_send = pack_q(queries[0], g, hl)
-    kv = lax.all_to_all(kv_send, axes, split_axis=0, concat_axis=0, tiled=True)
-    q = lax.all_to_all(q_send, axes, split_axis=0, concat_axis=0, tiled=True)
+    kv = lax.all_to_all(kv_send, ("lo", "mem"), split_axis=0, concat_axis=0, tiled=True)
+    q = lax.all_to_all(q_send, ("mem", "lo"), split_axis=0, concat_axis=0, tiled=True)
     state, total = local_state(kv, hl, memories, td)
     entering = entering_state(state, total, groups, hl, memories)
-    place = lax.axis_index("lo") * memories + lax.axis_index("mem")
-    own_gain = lax.dynamic_slice_in_dim(gain.reshape(heads, hd), place * hl, hl, 0)
-    lhs, factors = chunk_states(kv, hl, memories, td)
-    out = readout(q, kv, lhs, factors, entering, own_gain, hl, memories, td)
-    back = lax.all_to_all(out, axes, split_axis=0, concat_axis=0, tiled=True)
+    factors = chunk_factors(kv, hl, memories, td)
+    lhs = chunk_states(kv, factors, hl, memories, td)
+    out = readout(q, kv, lhs, factors, entering, gain.reshape(heads, hd), lo, hl, memories, td)
+    back = lax.all_to_all(out, ("mem", "lo"), split_axis=0, concat_axis=0, tiled=True)
     return back.reshape(heads, td, hd).transpose(1, 0, 2)[None]
 
 

time: 95.6 us -> 91.4 us (0.956)
  Pallas kernels: 23.3 us -> 20.2 us
  blocking collectives: 23 us -> 20.3 us
  waiting for transfers between devices: 31.4 us -> 33.7 us
  local copies, waits for them, and re-layouts: 2.96 us -> 1.66 us
    all_to_all x1, blocking collectives: 23 us -> 20.3 us  [shards(): lax.all_to_all(out, ('mem', 'lo'), split_axis=0, concat_axis=0, tiled=True)]
    pallas_call x3 -> x4, Pallas kernels: 16.9 us -> 14.9 us  [the longest x1 6.3 us: readout(): pl.pallas_call(functools.partial(readout_kernel, hl, memories, lo, td), g...]
    ppermute x1, waiting for transfers between devices: 1.97 us -> 3.66 us  [entering_state(): state = lax.ppermute(state, 'hi', [(i, i + 1) for i in range(groups - 1)])]
    broadcast_in_dim x0 -> x1, local copies, waits for them, and re-layouts: none -> 1.65 us  [shards(): return back.reshape(heads, td, hd).transpose(1, 0, 2)[None]]
    reshape x1 -> x0, local copies, waits for them, and re-layouts: 1.65 us -> none  [shards(): return back.reshape(heads, td, hd).transpose(1, 0, 2)[None]]
    pallas_call x1, Pallas kernels: 3.61 us -> 2.52 us  [local_state(): pl.pallas_call(functools.partial(state_kernel, g, hl, memories, td), grid...]
  transfers between devices with their start and end apart: 3 -> 3, of which waited for: 3 -> 3; matrix products, arithmetic and copies ran while one was open for 1% -> 0% of each run, Pallas kernels for 13% -> 11%
where the time goes in v3:
time: 91.4 us; the launch traced here: 91 us
  waiting for transfers between devices  33.7 us (37%)
  blocking collectives  20.3 us (22%)
  Pallas kernels  20.2 us (22%)
  starting transfers between devices  15.2 us (17%)
  local copies, waits for them, and re-layouts  1.66 us (2%)
    all_to_all x1, waiting for transfers between devices, shards(): lax.all_to_all(kv_send, ('lo', 'mem'), split_axis=0, concat_axis=0, tiled...  27.9 us
    all_to_all x1, blocking collectives, shards(): lax.all_to_all(out, ('mem', 'lo'), split_axis=0, concat_axis=0, tiled=True)  20.3 us
    all_to_all x1, starting transfers between devices, shards(): lax.all_to_all(kv_send, ('lo', 'mem'), split_axis=0, concat_axis=0, tiled...  6.32 us
    pallas_call x1, Pallas kernels, readout(): pl.pallas_call(functools.partial(readout_kernel, hl, memories, lo, td), g...  6.3 us
    ppermute x1, starting transfers between devices, entering_state(): state = lax.ppermute(state, 'hi', [(i, i + 1) for i in range(groups - 1)])  5.21 us
    pallas_call x1, Pallas kernels, chunk_states(): pl.pallas_call(functools.partial(chunk_kernel, hl, memories, td), grid=(g...  4.61 us
    pallas_call x1, Pallas kernels, pack_kv(): pl.pallas_call(functools.partial(pack_kv_kernel, hl, lo), grid=(heads //...  3.79 us
    all_to_all x1, starting transfers between devices, shards(): lax.all_to_all(q_send, ('mem', 'lo'), split_axis=0, concat_axis=0, tiled=...  3.69 us
  transfers between devices with their start and end apart: 3, of which 3 were waited for; matrix products, arithmetic and copies ran while one was open for 0% of the time, Pallas kernels for 11%

profile of v3, /device:TPU:0, one launch (start us, length us, event | category | flops | bytes accessed | tf_op | source)
XLA Modules:
  0.0 91.0 jit_solution(14334712560962186169)
XLA Ops:
  0.0 3.8 %pack_kv.1 = bf16[4,4,528,128]{3,2,1,0:T(8,128)(2,1)} custom-call(bf16[128,32,128]{2,1,0:T(8,128)(2,1)} %bitcast.31, bf16[128,32,128]{2,1,0:T(8,128)(2,1)} %bitcast.32, bf16[32,128]{1,0:T(8,128)(2,1)} %bitcast.33, s32[2,128]{1,0:T(2,128)} %bitcast.34, f32[2,128]{1,0:T(2,128)} %bitcast.35), custom_call_target="tpu_custom_call" | custom-call | tf_op jit(solution)/shard_map/pack_kv/pallas_call | solution.py:64
  3.8 6.3 %all-to-all-start.1 = ((bf16[16,528,128]{2,1,0:T(8,128)(2,1)}), bf16[16,528,128]{2,1,0:T(8,128)(2,1)S(1)}, u32[]{:S(2)}, u32[]{:S(2)}) async-start(bf16[16,528,128]{2,1,0:T(8,128)(2,1)} %bitcast.28), calls=%async_computation.1 | async-start | bytes 4325376 | tf_op jit(solution)/shard_map/all_to_all | solution.py:383
  10.1 2.7 %pack_q.1 = bf16[16,256,128]{2,1,0:T(8,128)(2,1)} custom-call(bf16[128,32,128]{2,1,0:T(8,128)(2,1)} %bitcast.30), custom_call_target="tpu_custom_call" | custom-call | tf_op jit(solution)/shard_map/pack_q/pallas_call | solution.py:78
  12.9 27.9 %all-to-all-done.1.meta_ref.kv_ref = bf16[16,528,128]{2,1,0:T(8,128)(2,1)S(1)} async-done(((bf16[16,528,128]{2,1,0:T(8,128)(2,1)}), bf16[16,528,128]{2,1,0:T(8,128)(2,1)S(1)}, u32[]{:S(2)}, u32[]{:S(2)}) %all-to-all-start.1) | async-done | bytes 2162720 | tf_op jit(solution)/shard_map/all_to_all | solution.py:383
  40.7 0.0 copy-start
  40.7 3.7 %all-to-all-start = ((bf16[16,256,128]{2,1,0:T(8,128)(2,1)}), bf16[16,256,128]{2,1,0:T(8,128)(2,1)S(1)}, u32[]{:S(2)}, u32[]{:S(2)}) async-start(bf16[16,256,128]{2,1,0:T(8,128)(2,1)} %pack_q.1), calls=%async_computation | async-start | bytes 2097152 | tf_op jit(solution)/shard_map/all_to_all | solution.py:384
  44.4 2.5 %local_state.1 = (bf16[2,512,128]{2,1,0:T(8,128)(2,1)}, f32[8,128]{1,0:T(8,128)}) custom-call(bf16[16,528,128]{2,1,0:T(8,128)(2,1)S(1)} %all-to-all-done.1.meta_ref.kv_ref, bf16[16,528,128]{2,1,0:T(8,128)(2,1)S(1)} %all-to-all-done.1.meta_ref.kv_ref), custom_call_target="tpu_custom_call" | custom-call | flops 536870912 | bytes 2162688 | tf_op jit(solution)/shard_map/local_state/pallas_call | solution.py:160
  46.9 5.2 %collective-permute-start = (bf16[2,512,128]{2,1,0:T(8,128)(2,1)}, bf16[2,512,128]{2,1,0:T(8,128)(2,1)}, u32[]{:S(2)}, u32[]{:S(2)}) collective-permute-start(bf16[2,512,128]{2,1,0:T(8,128)(2,1)} %get-tuple-element.6), channel_id=1, source_target_pairs={{0,4},{1,5},{2,6},{3,7},{8,12},{9,13},{10,14},{11,15},{16,20},{17,... | collective-permute-start | bytes 786440 | tf_op jit(solution)/shard_map/ppermute | solution.py:351
  52.1 0.2 chunk_factors.1.fac_ref
  52.3 0.0 copy-done
  52.3 0.0 copy-start.1
  52.4 4.6 %chunk_states.1 = bf16[16,2,512,256]{3,2,1,0:T(8,128)(2,1)} custom-call(f32[16,40,128]{2,1,0:T(8,128)S(1)} %chunk_factors.1.fac_ref, bf16[16,528,128]{2,1,0:T(8,128)(2,1)S(1)} %all-to-all-done.1.meta_ref.kv_ref), custom_call_target="tpu_custom_call" | custom-call | flops 536870912 | bytes 10813440 | tf_op jit(solution)/shard_map/chunk_states/pallas_call | solution.py:247
  57.0 2.2 %all-to-all-done = bf16[16,256,128]{2,1,0:T(8,128)(2,1)S(1)} async-done(((bf16[16,256,128]{2,1,0:T(8,128)(2,1)}), bf16[16,256,128]{2,1,0:T(8,128)(2,1)S(1)}, u32[]{:S(2)}, u32[]{:S(2)}) %all-to-all-start) | async-done | bytes 1048608 | tf_op jit(solution)/shard_map/all_to_all | solution.py:384
  59.1 3.7 %collective-permute-done.state_ref = bf16[2,512,128]{2,1,0:T(8,128)(2,1)} collective-permute-done((bf16[2,512,128]{2,1,0:T(8,128)(2,1)}, bf16[2,512,128]{2,1,0:T(8,128)(2,1)}, u32[]{:S(2)}, u32[]{:S(2)}) %collective-permute-start) | collective-permute-done | bytes 262176 | tf_op jit(solution)/shard_map/ppermute | solution.py:351
  62.8 0.0 copy-done.1
  62.8 6.3 %readout.1 = bf16[4,4,256,128]{3,2,1,0:T(8,128)(2,1)S(1)} custom-call(bf16[4,4,256,128]{3,2,1,0:T(8,128)(2,1)S(1)} %bitcast.24, bf16[4,4,528,128]{3,2,1,0:T(8,128)(2,1)} %bitcast.23, bf16[4,4,2,512,256]{4,3,2,1,0:T(8,128)(2,1)} %bitcast.27, f32[16,40,128]{2,1,0:T(8,128)S(1)} %chunk_factors.1.fac_ref, bf16[2,512,128]{2,1,0:T(8,128)(2,1)} %collective-permute-done.state_ref, ...), custom_call_target="tpu_custom_call" | custom-call | flops 2147483648 | bytes 10813440 | tf_op jit(solution)/shard_map/readout/pallas_call | solution.py:314
  69.1 20.3 %all_to_all.15 = bf16[16,256,128]{2,1,0:T(8,128)(2,1)S(1)} all-to-all(bf16[16,256,128]{2,1,0:T(8,128)(2,1)S(1)} %bitcast.25), channel_id=1, replica_groups=mesh['mem'=4,'hi'=2,'lo'=4] {'mem','lo'}, dimensions={0} | all-to-all | bytes 2097152 | tf_op jit(solution)/shard_map/all_to_all | solution.py:390
  89.4 1.6 %copy.8 = bf16[1,128,32,128]{3,2,1,0:T(8,128)(2,1)} copy(bf16[1,128,32,128]{3,1,2,0:T(8,128)(2,1)S(1)} %bitcast.29) | data formatting | bytes 2097152 | tf_op jit(solution)/shard_map/broadcast_in_dim | solution.py:391
Async XLA Ops:
  3.8 36.9 %all-to-all-start.1 = ((bf16[16,528,128]{2,1,0:T(8,128)(2,1)}), bf16[16,528,128]{2,1,0:T(8,128)(2,1)S(1)}, u32[]{:S(2)}, u32[]{:S(2)}) async-start(bf16[16,528,128]{2,1,0:T(8,128)(2,1)} %bitcast.28), calls=%async_computation.1 | async-start | bytes 4325376 | tf_op jit(solution)/shard_map/all_to_all | solution.py:383
  40.7 11.6 %copy-start = (bf16[16,528,128]{2,1,0:T(8,128)(2,1)}, bf16[16,528,128]{2,1,0:T(8,128)(2,1)S(1)}, u32[]{:S(2)}) copy-start(bf16[16,528,128]{2,1,0:T(8,128)(2,1)S(1)} %all-to-all-done.1.meta_ref.kv_ref) | copy-start | bytes 6488068
  40.7 18.4 %all-to-all-start = ((bf16[16,256,128]{2,1,0:T(8,128)(2,1)}), bf16[16,256,128]{2,1,0:T(8,128)(2,1)S(1)}, u32[]{:S(2)}, u32[]{:S(2)}) async-start(bf16[16,256,128]{2,1,0:T(8,128)(2,1)} %pack_q.1), calls=%async_computation | async-start | bytes 2097152 | tf_op jit(solution)/shard_map/all_to_all | solution.py:384
  46.9 15.8 %collective-permute-start = (bf16[2,512,128]{2,1,0:T(8,128)(2,1)}, bf16[2,512,128]{2,1,0:T(8,128)(2,1)}, u32[]{:S(2)}, u32[]{:S(2)}) collective-permute-start(bf16[2,512,128]{2,1,0:T(8,128)(2,1)} %get-tuple-element.6), channel_id=1, source_target_pairs={{0,4},{1,5},{2,6},{3,7},{8,12},{9,13},{10,14},{11,15},{16,20},{17,... | collective-permute-start | bytes 786440 | tf_op jit(solution)/shard_map/ppermute | solution.py:351
  52.3 10.4 %copy-start.1 = (f32[4096]{0:T(1024)S(1)}, f32[4096]{0:T(1024)}, u32[]{:S(2)}) copy-start(f32[4096]{0:T(1024)} %param.13) | copy-start | bytes 49156

commit v4 on v3

--- a/solution.py
+++ b/solution.py
@@ -29,7 +29,7 @@
         place(j // hl)[start : start + td, :] = rows.T if turned else rows
 
 
-def pack_kv_kernel(hl, lo, k_ref, v_ref, ld_ref, rt_ref, wt_ref, out, scr_k, scr_v, ld_scr):
+def pack_kernel(hl, lo, k_ref, v_ref, q_ref, ld_ref, rt_ref, wt_ref, out, q_out, scr_k, scr_v, scr_q, ld_scr):
     i = pl.program_id(0)
     td, hb, _ = k_ref.shape
     place = lambda dd: out.at[dd % lo, dd // lo]
@@ -40,6 +40,7 @@
 
     split_heads(k_ref, place, scr_k, hl, 0, False)
     split_heads(v_ref, place, scr_v, hl, hl * td, True)
+    split_heads(q_ref, lambda dd: q_out.at[dd], scr_q, hl, 0, True)
     w = wt_ref[...]
     hi = w.astype(BF16).astype(F32)
     mid = (w - hi).astype(BF16).astype(F32)
@@ -51,39 +52,27 @@
         place(dd)[2 * hl * td :, :] = jnp.concatenate([table, own], axis=0).astype(BF16)
 
 
-def pack_q_kernel(hl, q_ref, out, scr):
-    split_heads(q_ref, lambda dd: out.at[dd], scr, hl, 0, True)
-
-
-def pack_kv(keys, values, ld_t, routes_t, weight_t, lo, memories, hl):
+def pack(keys, values, queries, ld_t, routes_t, weight_t, lo, memories, hl):
     td, heads, hd = keys.shape
     hb = math.gcd(heads, 16)
     rows = 2 * hl * td + META
     whole = lambda a: pl.BlockSpec(a.shape, lambda i: (0,) * a.ndim)
     block = pl.BlockSpec((td, hb, hd), lambda i: (0, i, 0))
     return pl.pallas_call(
-        functools.partial(pack_kv_kernel, hl, lo),
+        functools.partial(pack_kernel, hl, lo),
         grid=(heads // hb,),
-        in_specs=[block, block, whole(ld_t), whole(routes_t), whole(weight_t)],
-        out_specs=pl.BlockSpec((lo, hb // hl // lo, rows, hd), lambda i: (0, i, 0, 0)),
-        out_shape=jax.ShapeDtypeStruct((lo, memories, rows, hd), BF16),
-        scratch_shapes=[pltpu.VMEM((td * hb, hd), F32)] * 2 + [pltpu.VMEM((heads, td), F32)],
-        name="pack_kv",
-    )(keys, values, ld_t, routes_t, weight_t)
-
-
-def pack_q(queries, g, hl):
-    td, heads, hd = queries.shape
-    hb = math.gcd(heads, 16)
-    return pl.pallas_call(
-        functools.partial(pack_q_kernel, hl),
-        grid=(heads // hb,),
-        in_specs=[pl.BlockSpec((td, hb, hd), lambda i: (0, i, 0))],
-        out_specs=pl.BlockSpec((hb // hl, hl * td, hd), lambda i: (i, 0, 0)),
-        out_shape=jax.ShapeDtypeStruct((g, hl * td, hd), BF16),
-        scratch_shapes=[pltpu.VMEM((td * hb, hd), F32)],
-        name="pack_q",
-    )(queries)
+        in_specs=[block, block, block, whole(ld_t), whole(routes_t), whole(weight_t)],
+        out_specs=[
+            pl.BlockSpec((lo, hb // hl // lo, rows, hd), lambda i: (0, i, 0, 0)),
+            pl.BlockSpec((hb // hl, hl * td, hd), lambda i: (i, 0, 0)),
+        ],
+        out_shape=[
+            jax.ShapeDtypeStruct((lo, memories, rows, hd), BF16),
+            jax.ShapeDtypeStruct((lo * memories, hl * td, hd), BF16),
+        ],
+        scratch_shapes=[pltpu.VMEM((td * hb, hd), F32)] * 3 + [pltpu.VMEM((heads, td), F32)],
+        name="pack",
+    )(keys, values, queries, ld_t, routes_t, weight_t)
 
 
 def meta_rows(meta_ref, s, hl, memories):
@@ -376,10 +365,18 @@
     groups = lax.axis_size("hi")
     g = memories * lo
     hl = heads // g
-    kv_send = pack_kv(
-        keys[0], values[0], log_decay[0].T, routes[0].T, route_weight[0].T, lo, memories, hl
-    ).reshape(g, 2 * hl * td + META, hd)
-    q_send = pack_q(queries[0], g, hl)
+    kv_send, q_send = pack(
+        keys[0],
+        values[0],
+        queries[0],
+        log_decay[0].T,
+        routes[0].T,
+        route_weight[0].T,
+        lo,
+        memories,
+        hl,
+    )
+    kv_send = kv_send.reshape(g, 2 * hl * td + META, hd)
     kv = lax.all_to_all(kv_send, ("lo", "mem"), split_axis=0, concat_axis=0, tiled=True)
     q = lax.all_to_all(q_send, ("mem", "lo"), split_axis=0, concat_axis=0, tiled=True)
     state, total = local_state(kv, hl, memories, td)

time: 91.4 us -> 89.9 us (0.984)
  blocking collectives: 20.3 us -> 55 us
  waiting for transfers between devices: 33.7 us -> 5.53 us
  starting transfers between devices: 15.2 us -> 8.85 us
  Pallas kernels: 20.2 us -> 18.5 us
    all_to_all x0 -> x1, blocking collectives: none -> 34.4 us  [shards(): lax.all_to_all(kv_send, ('lo', 'mem'), split_axis=0, concat_axis=0, tiled...]
    all_to_all x1 -> x0, waiting for transfers between devices: 27.9 us -> none  [shards(): lax.all_to_all(kv_send, ('lo', 'mem'), split_axis=0, concat_axis=0, tiled...]
    all_to_all x1 -> x0, starting transfers between devices: 6.32 us -> none  [shards(): lax.all_to_all(kv_send, ('lo', 'mem'), split_axis=0, concat_axis=0, tiled...]
    pallas_call x2 -> x1, Pallas kernels: 6.53 us -> 4.92 us  [pack(): pl.pallas_call(functools.partial(pack_kernel, hl, lo), grid=(heads // hb,...]
  transfers between devices with their start and end apart: 3 -> 2, of which waited for: 3 -> 2; matrix products, arithmetic and copies ran while one was open for 0% -> 0% of each run, Pallas kernels for 11% -> 8%
where the time goes in v4:
time: 89.9 us; the launch traced here: 89.6 us
  blocking collectives  55 us (61%)
  Pallas kernels  18.5 us (21%)
  starting transfers between devices  8.85 us (10%)
  waiting for transfers between devices  5.53 us (6%)
  local copies, waits for them, and re-layouts  1.66 us (2%)
    all_to_all x1, blocking collectives, shards(): lax.all_to_all(kv_send, ('lo', 'mem'), split_axis=0, concat_axis=0, tiled...  34.4 us
    all_to_all x1, blocking collectives, shards(): lax.all_to_all(out, ('mem', 'lo'), split_axis=0, concat_axis=0, tiled=True)  20.5 us
    pallas_call x1, Pallas kernels, readout(): pl.pallas_call(functools.partial(readout_kernel, hl, memories, lo, td), g...  6.29 us
    ppermute x1, starting transfers between devices, entering_state(): state = lax.ppermute(state, 'hi', [(i, i + 1) for i in range(groups - 1)])  5.2 us
    pallas_call x1, Pallas kernels, pack(): pl.pallas_call(functools.partial(pack_kernel, hl, lo), grid=(heads // hb,...  4.92 us
    pallas_call x1, Pallas kernels, chunk_states(): pl.pallas_call(functools.partial(chunk_kernel, hl, memories, td), grid=(g...  4.6 us
    all_to_all x1, starting transfers between devices, shards(): lax.all_to_all(q_send, ('mem', 'lo'), split_axis=0, concat_axis=0, tiled=...  3.66 us
    ppermute x1, waiting for transfers between devices, entering_state(): state = lax.ppermute(state, 'hi', [(i, i + 1) for i in range(groups - 1)])  3.41 us
  transfers between devices with their start and end apart: 2, of which 2 were waited for; matrix products, arithmetic and copies ran while one was open for 0% of the time, Pallas kernels for 8%

profile of v4, /device:TPU:0, one launch (start us, length us, event | category | flops | bytes accessed | tf_op | source)
XLA Modules:
  0.0 89.6 jit_solution(12650141294717719612)
XLA Ops:
  0.0 4.9 %pack.1 = (bf16[4,4,528,128]{3,2,1,0:T(8,128)(2,1)}, bf16[16,256,128]{2,1,0:T(8,128)(2,1)}) custom-call(bf16[128,32,128]{2,1,0:T(8,128)(2,1)} %bitcast.30, bf16[128,32,128]{2,1,0:T(8,128)(2,1)} %bitcast.31, bf16[128,32,128]{2,1,0:T(8,128)(2,1)} %bitcast.32, bf16[32,128]{1,0:T(8,128)(2,1)} %bitcast.33, s32[2,128]{1,0:T(2,128)} %bitcast.34, f32[2,128]{1,0:T(2,128)} %bitcast.35), custom_call_target="tpu_custom_call" | custom-call | tf_op jit(solution)/shard_map/pack/pallas_call | solution.py:61
  4.9 34.4 %all_to_all.15.meta_ref.kv_ref = bf16[16,528,128]{2,1,0:T(8,128)(2,1)S(1)} all-to-all(bf16[16,528,128]{2,1,0:T(8,128)(2,1)} %bitcast.29), channel_id=1, replica_groups=mesh['mem'=4,'hi'=2,'lo'=4] {'lo','mem'}, dimensions={0} | all-to-all | bytes 4325376 | tf_op jit(solution)/shard_map/all_to_all | solution.py:380
  39.3 0.0 copy-start
  39.3 3.7 %all-to-all-start = ((bf16[16,256,128]{2,1,0:T(8,128)(2,1)}), bf16[16,256,128]{2,1,0:T(8,128)(2,1)S(1)}, u32[]{:S(2)}, u32[]{:S(2)}) async-start(bf16[16,256,128]{2,1,0:T(8,128)(2,1)} %get-tuple-element.8), calls=%async_computation | async-start | bytes 2097152 | tf_op jit(solution)/shard_map/all_to_all | solution.py:381
  43.0 2.5 %local_state.1 = (bf16[2,512,128]{2,1,0:T(8,128)(2,1)}, f32[8,128]{1,0:T(8,128)}) custom-call(bf16[16,528,128]{2,1,0:T(8,128)(2,1)S(1)} %all_to_all.15.meta_ref.kv_ref, bf16[16,528,128]{2,1,0:T(8,128)(2,1)S(1)} %all_to_all.15.meta_ref.kv_ref), custom_call_target="tpu_custom_call" | custom-call | flops 536870912 | bytes 2162688 | tf_op jit(solution)/shard_map/local_state/pallas_call | solution.py:149
  45.5 5.2 %collective-permute-start = (bf16[2,512,128]{2,1,0:T(8,128)(2,1)}, bf16[2,512,128]{2,1,0:T(8,128)(2,1)}, u32[]{:S(2)}, u32[]{:S(2)}) collective-permute-start(bf16[2,512,128]{2,1,0:T(8,128)(2,1)} %get-tuple-element.10), channel_id=1, source_target_pairs={{0,4},{1,5},{2,6},{3,7},{8,12},{9,13},{10,14},{11,15},{16,20},{17,... | collective-permute-start | bytes 786440 | tf_op jit(solution)/shard_map/ppermute | solution.py:340
  50.7 0.2 chunk_factors.1.fac_ref
  50.9 0.0 copy-done
  50.9 0.0 copy-start.1
  50.9 4.6 %chunk_states.1 = bf16[16,2,512,256]{3,2,1,0:T(8,128)(2,1)} custom-call(f32[16,40,128]{2,1,0:T(8,128)S(1)} %chunk_factors.1.fac_ref, bf16[16,528,128]{2,1,0:T(8,128)(2,1)S(1)} %all_to_all.15.meta_ref.kv_ref), custom_call_target="tpu_custom_call" | custom-call | flops 536870912 | bytes 10813440 | tf_op jit(solution)/shard_map/chunk_states/pallas_call | solution.py:236
  55.5 2.1 %all-to-all-done = bf16[16,256,128]{2,1,0:T(8,128)(2,1)S(1)} async-done(((bf16[16,256,128]{2,1,0:T(8,128)(2,1)}), bf16[16,256,128]{2,1,0:T(8,128)(2,1)S(1)}, u32[]{:S(2)}, u32[]{:S(2)}) %all-to-all-start) | async-done | bytes 1048608 | tf_op jit(solution)/shard_map/all_to_all | solution.py:381
  57.7 3.4 %collective-permute-done.state_ref = bf16[2,512,128]{2,1,0:T(8,128)(2,1)} collective-permute-done((bf16[2,512,128]{2,1,0:T(8,128)(2,1)}, bf16[2,512,128]{2,1,0:T(8,128)(2,1)}, u32[]{:S(2)}, u32[]{:S(2)}) %collective-permute-start) | collective-permute-done | bytes 262176 | tf_op jit(solution)/shard_map/ppermute | solution.py:340
  61.1 0.0 copy-done.1
  61.1 6.3 %readout.1 = bf16[4,4,256,128]{3,2,1,0:T(8,128)(2,1)S(1)} custom-call(bf16[4,4,256,128]{3,2,1,0:T(8,128)(2,1)S(1)} %bitcast.24, bf16[4,4,528,128]{3,2,1,0:T(8,128)(2,1)} %bitcast.23, bf16[4,4,2,512,256]{4,3,2,1,0:T(8,128)(2,1)} %bitcast.27, f32[16,40,128]{2,1,0:T(8,128)S(1)} %chunk_factors.1.fac_ref, bf16[2,512,128]{2,1,0:T(8,128)(2,1)} %collective-permute-done.state_ref, ...), custom_call_target="tpu_custom_call" | custom-call | flops 2147483648 | bytes 10813440 | tf_op jit(solution)/shard_map/readout/pallas_call | solution.py:303
  67.4 20.5 %all_to_all.16 = bf16[16,256,128]{2,1,0:T(8,128)(2,1)S(1)} all-to-all(bf16[16,256,128]{2,1,0:T(8,128)(2,1)S(1)} %bitcast.25), channel_id=1, replica_groups=mesh['mem'=4,'hi'=2,'lo'=4] {'mem','lo'}, dimensions={0} | all-to-all | bytes 2097152 | tf_op jit(solution)/shard_map/all_to_all | solution.py:387
  87.9 1.6 %copy.8 = bf16[1,128,32,128]{3,2,1,0:T(8,128)(2,1)} copy(bf16[1,128,32,128]{3,1,2,0:T(8,128)(2,1)S(1)} %bitcast.28) | data formatting | bytes 2097152 | tf_op jit(solution)/shard_map/broadcast_in_dim | solution.py:388
Async XLA Ops:
  39.3 11.6 %copy-start = (bf16[16,528,128]{2,1,0:T(8,128)(2,1)}, bf16[16,528,128]{2,1,0:T(8,128)(2,1)S(1)}, u32[]{:S(2)}) copy-start(bf16[16,528,128]{2,1,0:T(8,128)(2,1)S(1)} %all_to_all.15.meta_ref.kv_ref) | copy-start | bytes 6488068
  39.3 18.3 %all-to-all-start = ((bf16[16,256,128]{2,1,0:T(8,128)(2,1)}), bf16[16,256,128]{2,1,0:T(8,128)(2,1)S(1)}, u32[]{:S(2)}, u32[]{:S(2)}) async-start(bf16[16,256,128]{2,1,0:T(8,128)(2,1)} %get-tuple-element.8), calls=%async_computation | async-start | bytes 2097152 | tf_op jit(solution)/shard_map/all_to_all | solution.py:381
  45.5 15.5 %collective-permute-start = (bf16[2,512,128]{2,1,0:T(8,128)(2,1)}, bf16[2,512,128]{2,1,0:T(8,128)(2,1)}, u32[]{:S(2)}, u32[]{:S(2)}) collective-permute-start(bf16[2,512,128]{2,1,0:T(8,128)(2,1)} %get-tuple-element.10), channel_id=1, source_target_pairs={{0,4},{1,5},{2,6},{3,7},{8,12},{9,13},{10,14},{11,15},{16,20},{17,... | collective-permute-start | bytes 786440 | tf_op jit(solution)/shard_map/ppermute | solution.py:340
  50.9 10.1 %copy-start.1 = (f32[4096]{0:T(1024)S(1)}, f32[4096]{0:T(1024)}, u32[]{:S(2)}) copy-start(f32[4096]{0:T(1024)} %param.13) | copy-start | bytes 49156

commit v5 on v4

--- a/solution.py
+++ b/solution.py
@@ -11,7 +11,8 @@
 
 F32 = jnp.float32
 BF16 = jnp.bfloat16
-META = 16
+META = 8
+RATES = 6
 PARAMS = pltpu.CompilerParams(vmem_limit_bytes=50 << 20)
 ROWS = 8
 
@@ -44,11 +45,10 @@
     w = wt_ref[...]
     hi = w.astype(BF16).astype(F32)
     mid = (w - hi).astype(BF16).astype(F32)
-    low = (w - hi) - mid
-    table = jnp.concatenate([rt_ref[...].astype(F32), hi, mid, low], axis=0)
+    table = jnp.concatenate([rt_ref[...].astype(F32), hi, mid], axis=0)
     here = ld_scr[pl.ds(pl.multiple_of(i * hb, hb), hb), :]
     for dd in range(hb // hl):
-        own = (here if dd == 0 else pltpu.roll(here, hb - dd * hl, 0))[: META - ROWS]
+        own = (here if dd == 0 else pltpu.roll(here, hb - dd * hl, 0))[: META - RATES]
         place(dd)[2 * hl * td :, :] = jnp.concatenate([table, own], axis=0).astype(BF16)
 
 
@@ -82,9 +82,9 @@
     memory = lax.rem(row, memories).astype(F32)
     first = meta[0:1] == memory
     second = meta[1:2] == memory
-    rate = jnp.broadcast_to(meta[8:9], (ROWS, td))
+    rate = jnp.broadcast_to(meta[RATES : RATES + 1], (ROWS, td))
     for h in range(1, hl):
-        rate = jnp.where(row >= h * memories, meta[8 + h : 9 + h], rate)
+        rate = jnp.where(row >= h * memories, meta[RATES + h : RATES + h + 1], rate)
     member = first | second
     return meta, first, second, member, jnp.where(member, rate, 0.0)
 
@@ -145,7 +145,7 @@
 
 def local_state(kv, hl, memories, td):
     g, rows, hd = kv.shape
-    step = math.gcd(g, 8)
+    step = math.gcd(g, 16)
     return pl.pallas_call(
         functools.partial(state_kernel, g, hl, memories, td),
         grid=(g // step,),
@@ -181,7 +181,7 @@
         rows = slice(s * ROWS, (s + 1) * ROWS)
         running, total = cs_scr[rows, :td], cs_scr[rows, td:]
         half = 0.5 * total
-        weight = [meta[2 + n : 3 + n] + (meta[4 + n : 5 + n] + meta[6 + n : 7 + n]) for n in range(2)]
+        weight = [meta[2 + n : 3 + n] + meta[4 + n : 5 + n] for n in range(2)]
         fac_ref[s, 0:ROWS, :] = jnp.exp(running - half) * scale
         fac_ref[s, ROWS : 2 * ROWS, :] = jnp.where(first, weight[0], 0.0) + jnp.where(
             second, weight[1], 0.0
@@ -365,6 +365,7 @@
     groups = lax.axis_size("hi")
     g = memories * lo
     hl = heads // g
+    assert hl <= META - RATES and hl * memories == ROWS
     kv_send, q_send = pack(
         keys[0],
         values[0],

time: 89.9 us -> 89.2 us (level)
  no operation moved by 1% of the time
where the time goes in v5:
time: 89.2 us; the launch traced here: 88.9 us
  blocking collectives  54.3 us (61%)
  Pallas kernels  18.2 us (20%)
  starting transfers between devices  8.84 us (10%)
  waiting for transfers between devices  5.89 us (7%)
  local copies, waits for them, and re-layouts  1.66 us (2%)
    all_to_all x1, blocking collectives, shards(): lax.all_to_all(kv_send, ('lo', 'mem'), split_axis=0, concat_axis=0, tiled...  34.1 us
    all_to_all x1, blocking collectives, shards(): lax.all_to_all(out, ('mem', 'lo'), split_axis=0, concat_axis=0, tiled=True)  20.2 us
    pallas_call x1, Pallas kernels, readout(): pl.pallas_call(functools.partial(readout_kernel, hl, memories, lo, td), g...  6.3 us
    ppermute x1, starting transfers between devices, entering_state(): state = lax.ppermute(state, 'hi', [(i, i + 1) for i in range(groups - 1)])  5.19 us
    pallas_call x1, Pallas kernels, pack(): pl.pallas_call(functools.partial(pack_kernel, hl, lo), grid=(heads // hb,...  4.9 us
    pallas_call x1, Pallas kernels, chunk_states(): pl.pallas_call(functools.partial(chunk_kernel, hl, memories, td), grid=(g...  4.6 us
    all_to_all x1, starting transfers between devices, shards(): lax.all_to_all(q_send, ('mem', 'lo'), split_axis=0, concat_axis=0, tiled=...  3.66 us
    ppermute x1, waiting for transfers between devices, entering_state(): state = lax.ppermute(state, 'hi', [(i, i + 1) for i in range(groups - 1)])  3.41 us
  transfers between devices with their start and end apart: 2, of which 2 were waited for; matrix products, arithmetic and copies ran while one was open for 0% of the time, Pallas kernels for 8%

profile of v5, /device:TPU:0, one launch (start us, length us, event | category | flops | bytes accessed | tf_op | source)
XLA Modules:
  0.0 88.9 jit_solution(14721715300032950046)
XLA Ops:
  0.0 4.9 %pack.1 = (bf16[4,4,520,128]{3,2,1,0:T(8,128)(2,1)}, bf16[16,256,128]{2,1,0:T(8,128)(2,1)}) custom-call(bf16[128,32,128]{2,1,0:T(8,128)(2,1)} %bitcast.30, bf16[128,32,128]{2,1,0:T(8,128)(2,1)} %bitcast.31, bf16[128,32,128]{2,1,0:T(8,128)(2,1)} %bitcast.32, bf16[32,128]{1,0:T(8,128)(2,1)} %bitcast.33, s32[2,128]{1,0:T(2,128)} %bitcast.34, f32[2,128]{1,0:T(2,128)} %bitcast.35), custom_call_target="tpu_custom_call" | custom-call | tf_op jit(solution)/shard_map/pack/pallas_call | solution.py:61
  4.9 34.1 %all_to_all.15.meta_ref.kv_ref = bf16[16,520,128]{2,1,0:T(8,128)(2,1)S(1)} all-to-all(bf16[16,520,128]{2,1,0:T(8,128)(2,1)} %bitcast.29), channel_id=1, replica_groups=mesh['mem'=4,'hi'=2,'lo'=4] {'lo','mem'}, dimensions={0} | all-to-all | bytes 4259840 | tf_op jit(solution)/shard_map/all_to_all | solution.py:381
  39.0 0.0 copy-start
  39.0 3.7 %all-to-all-start = ((bf16[16,256,128]{2,1,0:T(8,128)(2,1)}), bf16[16,256,128]{2,1,0:T(8,128)(2,1)S(1)}, u32[]{:S(2)}, u32[]{:S(2)}) async-start(bf16[16,256,128]{2,1,0:T(8,128)(2,1)} %get-tuple-element.8), calls=%async_computation | async-start | bytes 2097152 | tf_op jit(solution)/shard_map/all_to_all | solution.py:382
  42.6 2.2 %local_state.1 = (bf16[2,512,128]{2,1,0:T(8,128)(2,1)}, f32[8,128]{1,0:T(8,128)}) custom-call(bf16[16,520,128]{2,1,0:T(8,128)(2,1)S(1)} %all_to_all.15.meta_ref.kv_ref, bf16[16,520,128]{2,1,0:T(8,128)(2,1)S(1)} %all_to_all.15.meta_ref.kv_ref), custom_call_target="tpu_custom_call" | custom-call | flops 536870912 | bytes 2129920 | tf_op jit(solution)/shard_map/local_state/pallas_call | solution.py:149
  44.8 5.2 %collective-permute-start = (bf16[2,512,128]{2,1,0:T(8,128)(2,1)}, bf16[2,512,128]{2,1,0:T(8,128)(2,1)}, u32[]{:S(2)}, u32[]{:S(2)}) collective-permute-start(bf16[2,512,128]{2,1,0:T(8,128)(2,1)} %get-tuple-element.10), channel_id=1, source_target_pairs={{0,4},{1,5},{2,6},{3,7},{8,12},{9,13},{10,14},{11,15},{16,20},{17,... | collective-permute-start | bytes 786440 | tf_op jit(solution)/shard_map/ppermute | solution.py:340
  50.0 0.2 chunk_factors.1.fac_ref
  50.2 0.0 copy-done
  50.2 0.0 copy-start.1
  50.2 4.6 %chunk_states.1 = bf16[16,2,512,256]{3,2,1,0:T(8,128)(2,1)} custom-call(f32[16,40,128]{2,1,0:T(8,128)S(1)} %chunk_factors.1.fac_ref, bf16[16,520,128]{2,1,0:T(8,128)(2,1)S(1)} %all_to_all.15.meta_ref.kv_ref), custom_call_target="tpu_custom_call" | custom-call | flops 536870912 | bytes 10649600 | tf_op jit(solution)/shard_map/chunk_states/pallas_call | solution.py:236
  54.8 2.5 %all-to-all-done = bf16[16,256,128]{2,1,0:T(8,128)(2,1)S(1)} async-done(((bf16[16,256,128]{2,1,0:T(8,128)(2,1)}), bf16[16,256,128]{2,1,0:T(8,128)(2,1)S(1)}, u32[]{:S(2)}, u32[]{:S(2)}) %all-to-all-start) | async-done | bytes 1048608 | tf_op jit(solution)/shard_map/all_to_all | solution.py:382
  57.3 3.4 %collective-permute-done.state_ref = bf16[2,512,128]{2,1,0:T(8,128)(2,1)} collective-permute-done((bf16[2,512,128]{2,1,0:T(8,128)(2,1)}, bf16[2,512,128]{2,1,0:T(8,128)(2,1)}, u32[]{:S(2)}, u32[]{:S(2)}) %collective-permute-start) | collective-permute-done | bytes 262176 | tf_op jit(solution)/shard_map/ppermute | solution.py:340
  60.7 0.0 copy-done.1
  60.7 6.3 %readout.1 = bf16[4,4,256,128]{3,2,1,0:T(8,128)(2,1)S(1)} custom-call(bf16[4,4,256,128]{3,2,1,0:T(8,128)(2,1)S(1)} %bitcast.24, bf16[4,4,520,128]{3,2,1,0:T(8,128)(2,1)} %bitcast.23, bf16[4,4,2,512,256]{4,3,2,1,0:T(8,128)(2,1)} %bitcast.27, f32[16,40,128]{2,1,0:T(8,128)S(1)} %chunk_factors.1.fac_ref, bf16[2,512,128]{2,1,0:T(8,128)(2,1)} %collective-permute-done.state_ref, ...), custom_call_target="tpu_custom_call" | custom-call | flops 2147483648 | bytes 10649600 | tf_op jit(solution)/shard_map/readout/pallas_call | solution.py:303
  67.0 20.2 %all_to_all.16 = bf16[16,256,128]{2,1,0:T(8,128)(2,1)S(1)} all-to-all(bf16[16,256,128]{2,1,0:T(8,128)(2,1)S(1)} %bitcast.25), channel_id=1, replica_groups=mesh['mem'=4,'hi'=2,'lo'=4] {'mem','lo'}, dimensions={0} | all-to-all | bytes 2097152 | tf_op jit(solution)/shard_map/all_to_all | solution.py:388
  87.2 1.6 %copy.8 = bf16[1,128,32,128]{3,2,1,0:T(8,128)(2,1)} copy(bf16[1,128,32,128]{3,1,2,0:T(8,128)(2,1)S(1)} %bitcast.28) | data formatting | bytes 2097152 | tf_op jit(solution)/shard_map/broadcast_in_dim | solution.py:389
Async XLA Ops:
  39.0 11.2 %copy-start = (bf16[16,520,128]{2,1,0:T(8,128)(2,1)}, bf16[16,520,128]{2,1,0:T(8,128)(2,1)S(1)}, u32[]{:S(2)}) copy-start(bf16[16,520,128]{2,1,0:T(8,128)(2,1)S(1)} %all_to_all.15.meta_ref.kv_ref) | copy-start | bytes 6389764
  39.0 18.3 %all-to-all-start = ((bf16[16,256,128]{2,1,0:T(8,128)(2,1)}), bf16[16,256,128]{2,1,0:T(8,128)(2,1)S(1)}, u32[]{:S(2)}, u32[]{:S(2)}) async-start(bf16[16,256,128]{2,1,0:T(8,128)(2,1)} %get-tuple-element.8), calls=%async_computation | async-start | bytes 2097152 | tf_op jit(solution)/shard_map/all_to_all | solution.py:382
  44.8 15.9 %collective-permute-start = (bf16[2,512,128]{2,1,0:T(8,128)(2,1)}, bf16[2,512,128]{2,1,0:T(8,128)(2,1)}, u32[]{:S(2)}, u32[]{:S(2)}) collective-permute-start(bf16[2,512,128]{2,1,0:T(8,128)(2,1)} %get-tuple-element.10), channel_id=1, source_target_pairs={{0,4},{1,5},{2,6},{3,7},{8,12},{9,13},{10,14},{11,15},{16,20},{17,... | collective-permute-start | bytes 786440 | tf_op jit(solution)/shard_map/ppermute | solution.py:340
  50.2 10.5 %copy-start.1 = (f32[4096]{0:T(1024)S(1)}, f32[4096]{0:T(1024)}, u32[]{:S(2)}) copy-start(f32[4096]{0:T(1024)} %param.13) | copy-start | bytes 49156

commit v6 on v5

--- a/solution.py
+++ b/solution.py
@@ -119,7 +119,8 @@
             )
             after = after + total
         total_ref[...] = jnp.exp(after)
-        acc_scr[...] = jnp.zeros_like(acc_scr)
+        if step < g:
+            acc_scr[...] = jnp.zeros_like(acc_scr)
 
     decay = dec_scr[i]
     for h in range(hl):
@@ -129,11 +130,18 @@
         ).astype(F32)
         for m in range(memories):
             j = h * memories + m
-            acc_scr[h, m * hd : (m + 1) * hd, :] += dot((value * decay[j : j + 1, :]).astype(BF16), key)
-
-    @pl.when(i == pl.num_programs(0) - 1)
-    def _():
-        state_ref[...] = acc_scr[...].astype(BF16)
+            rows = slice(m * hd, (m + 1) * hd)
+            grown = dot((value * decay[j : j + 1, :]).astype(BF16), key)
+            if step == g:
+                state_ref[h, rows, :] = grown.astype(BF16)
+            else:
+                acc_scr[h, rows, :] += grown
+
+    if step < g:
+
+        @pl.when(i == pl.num_programs(0) - 1)
+        def _():
+            state_ref[...] = acc_scr[...].astype(BF16)
 
 
 def chunk_specs(kv, hl, td, step):

time: 89.2 us -> 89.2 us (level)
  no operation moved by 1% of the time
where the time goes in v6:
time: 89.2 us; the launch traced here: 88.9 us
  blocking collectives  54.3 us (61%)
  Pallas kernels  18.2 us (20%)
  starting transfers between devices  8.84 us (10%)
  waiting for transfers between devices  5.89 us (7%)
  local copies, waits for them, and re-layouts  1.66 us (2%)
    all_to_all x1, blocking collectives, shards(): lax.all_to_all(kv_send, ('lo', 'mem'), split_axis=0, concat_axis=0, tiled...  34.1 us
    all_to_all x1, blocking collectives, shards(): lax.all_to_all(out, ('mem', 'lo'), split_axis=0, concat_axis=0, tiled=True)  20.2 us
    pallas_call x1, Pallas kernels, readout(): pl.pallas_call(functools.partial(readout_kernel, hl, memories, lo, td), g...  6.3 us
    ppermute x1, starting transfers between devices, entering_state(): state = lax.ppermute(state, 'hi', [(i, i + 1) for i in range(groups - 1)])  5.19 us
    pallas_call x1, Pallas kernels, pack(): pl.pallas_call(functools.partial(pack_kernel, hl, lo), grid=(heads // hb,...  4.9 us
    pallas_call x1, Pallas kernels, chunk_states(): pl.pallas_call(functools.partial(chunk_kernel, hl, memories, td), grid=(g...  4.6 us
    all_to_all x1, starting transfers between devices, shards(): lax.all_to_all(q_send, ('mem', 'lo'), split_axis=0, concat_axis=0, tiled=...  3.66 us
    ppermute x1, waiting for transfers between devices, entering_state(): state = lax.ppermute(state, 'hi', [(i, i + 1) for i in range(groups - 1)])  3.41 us
  transfers between devices with their start and end apart: 2, of which 2 were waited for; matrix products, arithmetic and copies ran while one was open for 0% of the time, Pallas kernels for 8%

profile of v6, /device:TPU:0, one launch (start us, length us, event | category | flops | bytes accessed | tf_op | source)
XLA Modules:
  0.0 88.9 jit_solution(14721715300032950046)
XLA Ops:
  0.0 4.9 %pack.1 = (bf16[4,4,520,128]{3,2,1,0:T(8,128)(2,1)}, bf16[16,256,128]{2,1,0:T(8,128)(2,1)}) custom-call(bf16[128,32,128]{2,1,0:T(8,128)(2,1)} %bitcast.30, bf16[128,32,128]{2,1,0:T(8,128)(2,1)} %bitcast.31, bf16[128,32,128]{2,1,0:T(8,128)(2,1)} %bitcast.32, bf16[32,128]{1,0:T(8,128)(2,1)} %bitcast.33, s32[2,128]{1,0:T(2,128)} %bitcast.34, f32[2,128]{1,0:T(2,128)} %bitcast.35), custom_call_target="tpu_custom_call" | custom-call | tf_op jit(solution)/shard_map/pack/pallas_call | solution.py:61
  4.9 34.1 %all_to_all.15.meta_ref.kv_ref = bf16[16,520,128]{2,1,0:T(8,128)(2,1)S(1)} all-to-all(bf16[16,520,128]{2,1,0:T(8,128)(2,1)} %bitcast.29), channel_id=1, replica_groups=mesh['mem'=4,'hi'=2,'lo'=4] {'lo','mem'}, dimensions={0} | all-to-all | bytes 4259840 | tf_op jit(solution)/shard_map/all_to_all | solution.py:389
  39.0 0.0 copy-start
  39.0 3.7 %all-to-all-start = ((bf16[16,256,128]{2,1,0:T(8,128)(2,1)}), bf16[16,256,128]{2,1,0:T(8,128)(2,1)S(1)}, u32[]{:S(2)}, u32[]{:S(2)}) async-start(bf16[16,256,128]{2,1,0:T(8,128)(2,1)} %get-tuple-element.8), calls=%async_computation | async-start | bytes 2097152 | tf_op jit(solution)/shard_map/all_to_all | solution.py:390
  42.6 2.2 %local_state.1 = (bf16[2,512,128]{2,1,0:T(8,128)(2,1)}, f32[8,128]{1,0:T(8,128)}) custom-call(bf16[16,520,128]{2,1,0:T(8,128)(2,1)S(1)} %all_to_all.15.meta_ref.kv_ref, bf16[16,520,128]{2,1,0:T(8,128)(2,1)S(1)} %all_to_all.15.meta_ref.kv_ref), custom_call_target="tpu_custom_call" | custom-call | flops 536870912 | bytes 2129920 | tf_op jit(solution)/shard_map/local_state/pallas_call | solution.py:157
  44.8 5.2 %collective-permute-start = (bf16[2,512,128]{2,1,0:T(8,128)(2,1)}, bf16[2,512,128]{2,1,0:T(8,128)(2,1)}, u32[]{:S(2)}, u32[]{:S(2)}) collective-permute-start(bf16[2,512,128]{2,1,0:T(8,128)(2,1)} %get-tuple-element.10), channel_id=1, source_target_pairs={{0,4},{1,5},{2,6},{3,7},{8,12},{9,13},{10,14},{11,15},{16,20},{17,... | collective-permute-start | bytes 786440 | tf_op jit(solution)/shard_map/ppermute | solution.py:348
  50.0 0.2 chunk_factors.1.fac_ref
  50.2 0.0 copy-done
  50.2 0.0 copy-start.1
  50.2 4.6 %chunk_states.1 = bf16[16,2,512,256]{3,2,1,0:T(8,128)(2,1)} custom-call(f32[16,40,128]{2,1,0:T(8,128)S(1)} %chunk_factors.1.fac_ref, bf16[16,520,128]{2,1,0:T(8,128)(2,1)S(1)} %all_to_all.15.meta_ref.kv_ref), custom_call_target="tpu_custom_call" | custom-call | flops 536870912 | bytes 10649600 | tf_op jit(solution)/shard_map/chunk_states/pallas_call | solution.py:244
  54.8 2.5 %all-to-all-done = bf16[16,256,128]{2,1,0:T(8,128)(2,1)S(1)} async-done(((bf16[16,256,128]{2,1,0:T(8,128)(2,1)}), bf16[16,256,128]{2,1,0:T(8,128)(2,1)S(1)}, u32[]{:S(2)}, u32[]{:S(2)}) %all-to-all-start) | async-done | bytes 1048608 | tf_op jit(solution)/shard_map/all_to_all | solution.py:390
  57.3 3.4 %collective-permute-done.state_ref = bf16[2,512,128]{2,1,0:T(8,128)(2,1)} collective-permute-done((bf16[2,512,128]{2,1,0:T(8,128)(2,1)}, bf16[2,512,128]{2,1,0:T(8,128)(2,1)}, u32[]{:S(2)}, u32[]{:S(2)}) %collective-permute-start) | collective-permute-done | bytes 262176 | tf_op jit(solution)/shard_map/ppermute | solution.py:348
  60.7 0.0 copy-done.1
  60.7 6.3 %readout.1 = bf16[4,4,256,128]{3,2,1,0:T(8,128)(2,1)S(1)} custom-call(bf16[4,4,256,128]{3,2,1,0:T(8,128)(2,1)S(1)} %bitcast.24, bf16[4,4,520,128]{3,2,1,0:T(8,128)(2,1)} %bitcast.23, bf16[4,4,2,512,256]{4,3,2,1,0:T(8,128)(2,1)} %bitcast.27, f32[16,40,128]{2,1,0:T(8,128)S(1)} %chunk_factors.1.fac_ref, bf16[2,512,128]{2,1,0:T(8,128)(2,1)} %collective-permute-done.state_ref, ...), custom_call_target="tpu_custom_call" | custom-call | flops 2147483648 | bytes 10649600 | tf_op jit(solution)/shard_map/readout/pallas_call | solution.py:311
  67.0 20.2 %all_to_all.16 = bf16[16,256,128]{2,1,0:T(8,128)(2,1)S(1)} all-to-all(bf16[16,256,128]{2,1,0:T(8,128)(2,1)S(1)} %bitcast.25), channel_id=1, replica_groups=mesh['mem'=4,'hi'=2,'lo'=4] {'mem','lo'}, dimensions={0} | all-to-all | bytes 2097152 | tf_op jit(solution)/shard_map/all_to_all | solution.py:396
  87.2 1.6 %copy.8 = bf16[1,128,32,128]{3,2,1,0:T(8,128)(2,1)} copy(bf16[1,128,32,128]{3,1,2,0:T(8,128)(2,1)S(1)} %bitcast.28) | data formatting | bytes 2097152 | tf_op jit(solution)/shard_map/broadcast_in_dim | solution.py:397
Async XLA Ops:
  39.0 11.2 %copy-start = (bf16[16,520,128]{2,1,0:T(8,128)(2,1)}, bf16[16,520,128]{2,1,0:T(8,128)(2,1)S(1)}, u32[]{:S(2)}) copy-start(bf16[16,520,128]{2,1,0:T(8,128)(2,1)S(1)} %all_to_all.15.meta_ref.kv_ref) | copy-start | bytes 6389764
  39.0 18.3 %all-to-all-start = ((bf16[16,256,128]{2,1,0:T(8,128)(2,1)}), bf16[16,256,128]{2,1,0:T(8,128)(2,1)S(1)}, u32[]{:S(2)}, u32[]{:S(2)}) async-start(bf16[16,256,128]{2,1,0:T(8,128)(2,1)} %get-tuple-element.8), calls=%async_computation | async-start | bytes 2097152 | tf_op jit(solution)/shard_map/all_to_all | solution.py:390
  44.8 15.9 %collective-permute-start = (bf16[2,512,128]{2,1,0:T(8,128)(2,1)}, bf16[2,512,128]{2,1,0:T(8,128)(2,1)}, u32[]{:S(2)}, u32[]{:S(2)}) collective-permute-start(bf16[2,512,128]{2,1,0:T(8,128)(2,1)} %get-tuple-element.10), channel_id=1, source_target_pairs={{0,4},{1,5},{2,6},{3,7},{8,12},{9,13},{10,14},{11,15},{16,20},{17,... | collective-permute-start | bytes 786440 | tf_op jit(solution)/shard_map/ppermute | solution.py:348
  50.2 10.5 %copy-start.1 = (f32[4096]{0:T(1024)S(1)}, f32[4096]{0:T(1024)}, u32[]{:S(2)}) copy-start(f32[4096]{0:T(1024)} %param.13) | copy-start | bytes 49156

commit v7 on v6

--- a/solution.py
+++ b/solution.py
@@ -277,13 +277,17 @@
 
     causal = lax.broadcasted_iota(jnp.int32, (td, td), 0) <= lax.broadcasted_iota(jnp.int32, (td, td), 1)
     units = [(a, b, h) for b in range(lo) for a in range(part) for h in range(hl)]
-    right = []
-    for a, b, h in units:
+    right = {}
+
+    def score(u):
+        a, b, h = units[u]
         query = q_ref[a, b, h * td : (h + 1) * td, :]
         key = k_ref[b, a, h * td : (h + 1) * td, :]
         scores = jnp.where(causal, dot(key, query), 0.0).astype(BF16)
-        right.append(jnp.concatenate([scores, query], axis=0))
-    for u, (a, b, h) in enumerate(units):
+        right[u] = jnp.concatenate([scores, query], axis=0)
+
+    def gather(u):
+        a, b, h = units[u]
         s = b * memories + i * part + a
         for m in range(memories):
             j = 2 * ROWS + h * memories + m
@@ -291,7 +295,9 @@
             state = lhs_ref[b, a, h, rows, td:].astype(F32) + st_scr[h, rows, :] * fac_ref[s, j : j + 1, :]
             left = jnp.concatenate([lhs_ref[b, a, h, rows, :td], state.astype(BF16)], axis=1)
             acc_scr[u, rows, :] = dot(left, right[u])
-    for u, (a, b, h) in enumerate(units):
+
+    def finish(u):
+        a, b, h = units[u]
         s = b * memories + i * part + a
         mixed = None
         for m in range(memories):
@@ -301,6 +307,15 @@
             term = read * (lax.rsqrt(mean + 1e-06) * fac_ref[s, ROWS + j : ROWS + j + 1, :])
             mixed = term if mixed is None else mixed + term
         out_ref[a, b, h * td : (h + 1) * td, :] = (mixed * gain_scr[h]).astype(BF16).T
+
+    count = len(units)
+    for u in range(count + 8):
+        if u < count:
+            score(u)
+        if 0 <= u - 4 < count:
+            gather(u - 4)
+        if 0 <= u - 8 < count:
+            finish(u - 8)
 
 
 def readout(q, kv, lhs, factors, state, gain, lo, hl, memories, td):

time: 89.2 us -> 89.2 us (level)
  no operation moved by 1% of the time
where the time goes in v7:
time: 89.2 us; the launch traced here: 88.9 us
  blocking collectives  54.2 us (61%)
  Pallas kernels  18.2 us (20%)
  starting transfers between devices  8.84 us (10%)
  waiting for transfers between devices  5.89 us (7%)
  local copies, waits for them, and re-layouts  1.66 us (2%)
    all_to_all x1, blocking collectives, shards(): lax.all_to_all(kv_send, ('lo', 'mem'), split_axis=0, concat_axis=0, tiled...  34.1 us
    all_to_all x1, blocking collectives, shards(): lax.all_to_all(out, ('mem', 'lo'), split_axis=0, concat_axis=0, tiled=True)  20.2 us
    pallas_call x1, Pallas kernels, readout(): pl.pallas_call(functools.partial(readout_kernel, hl, memories, lo, td), g...  6.37 us
    ppermute x1, starting transfers between devices, entering_state(): state = lax.ppermute(state, 'hi', [(i, i + 1) for i in range(groups - 1)])  5.19 us
    pallas_call x1, Pallas kernels, pack(): pl.pallas_call(functools.partial(pack_kernel, hl, lo), grid=(heads // hb,...  4.9 us
    pallas_call x1, Pallas kernels, chunk_states(): pl.pallas_call(functools.partial(chunk_kernel, hl, memories, td), grid=(g...  4.6 us
    all_to_all x1, starting transfers between devices, shards(): lax.all_to_all(q_send, ('mem', 'lo'), split_axis=0, concat_axis=0, tiled=...  3.66 us
    ppermute x1, waiting for transfers between devices, entering_state(): state = lax.ppermute(state, 'hi', [(i, i + 1) for i in range(groups - 1)])  3.41 us
  transfers between devices with their start and end apart: 2, of which 2 were waited for; matrix products, arithmetic and copies ran while one was open for 0% of the time, Pallas kernels for 8%

profile of v7, /device:TPU:0, one launch (start us, length us, event | category | flops | bytes accessed | tf_op | source)
XLA Modules:
  0.0 88.9 jit_solution(11924795232188696965)
XLA Ops:
  0.0 4.9 %pack.1 = (bf16[4,4,520,128]{3,2,1,0:T(8,128)(2,1)}, bf16[16,256,128]{2,1,0:T(8,128)(2,1)}) custom-call(bf16[128,32,128]{2,1,0:T(8,128)(2,1)} %bitcast.30, bf16[128,32,128]{2,1,0:T(8,128)(2,1)} %bitcast.31, bf16[128,32,128]{2,1,0:T(8,128)(2,1)} %bitcast.32, bf16[32,128]{1,0:T(8,128)(2,1)} %bitcast.33, s32[2,128]{1,0:T(2,128)} %bitcast.34, f32[2,128]{1,0:T(2,128)} %bitcast.35), custom_call_target="tpu_custom_call" | custom-call | tf_op jit(solution)/shard_map/pack/pallas_call | solution.py:61
  4.9 34.1 %all_to_all.15.meta_ref.kv_ref = bf16[16,520,128]{2,1,0:T(8,128)(2,1)S(1)} all-to-all(bf16[16,520,128]{2,1,0:T(8,128)(2,1)} %bitcast.29), channel_id=1, replica_groups=mesh['mem'=4,'hi'=2,'lo'=4] {'lo','mem'}, dimensions={0} | all-to-all | bytes 4259840 | tf_op jit(solution)/shard_map/all_to_all | solution.py:404
  39.0 0.0 copy-start
  39.0 3.7 %all-to-all-start = ((bf16[16,256,128]{2,1,0:T(8,128)(2,1)}), bf16[16,256,128]{2,1,0:T(8,128)(2,1)S(1)}, u32[]{:S(2)}, u32[]{:S(2)}) async-start(bf16[16,256,128]{2,1,0:T(8,128)(2,1)} %get-tuple-element.8), calls=%async_computation | async-start | bytes 2097152 | tf_op jit(solution)/shard_map/all_to_all | solution.py:405
  42.6 2.2 %local_state.1 = (bf16[2,512,128]{2,1,0:T(8,128)(2,1)}, f32[8,128]{1,0:T(8,128)}) custom-call(bf16[16,520,128]{2,1,0:T(8,128)(2,1)S(1)} %all_to_all.15.meta_ref.kv_ref, bf16[16,520,128]{2,1,0:T(8,128)(2,1)S(1)} %all_to_all.15.meta_ref.kv_ref), custom_call_target="tpu_custom_call" | custom-call | flops 536870912 | bytes 2129920 | tf_op jit(solution)/shard_map/local_state/pallas_call | solution.py:157
  44.8 5.2 %collective-permute-start = (bf16[2,512,128]{2,1,0:T(8,128)(2,1)}, bf16[2,512,128]{2,1,0:T(8,128)(2,1)}, u32[]{:S(2)}, u32[]{:S(2)}) collective-permute-start(bf16[2,512,128]{2,1,0:T(8,128)(2,1)} %get-tuple-element.10), channel_id=1, source_target_pairs={{0,4},{1,5},{2,6},{3,7},{8,12},{9,13},{10,14},{11,15},{16,20},{17,... | collective-permute-start | bytes 786440 | tf_op jit(solution)/shard_map/ppermute | solution.py:363
  50.0 0.2 chunk_factors.1.fac_ref
  50.2 0.0 copy-done
  50.2 0.0 copy-start.1
  50.2 4.6 %chunk_states.1 = bf16[16,2,512,256]{3,2,1,0:T(8,128)(2,1)} custom-call(f32[16,40,128]{2,1,0:T(8,128)S(1)} %chunk_factors.1.fac_ref, bf16[16,520,128]{2,1,0:T(8,128)(2,1)S(1)} %all_to_all.15.meta_ref.kv_ref), custom_call_target="tpu_custom_call" | custom-call | flops 536870912 | bytes 10649600 | tf_op jit(solution)/shard_map/chunk_states/pallas_call | solution.py:244
  54.8 2.5 %all-to-all-done = bf16[16,256,128]{2,1,0:T(8,128)(2,1)S(1)} async-done(((bf16[16,256,128]{2,1,0:T(8,128)(2,1)}), bf16[16,256,128]{2,1,0:T(8,128)(2,1)S(1)}, u32[]{:S(2)}, u32[]{:S(2)}) %all-to-all-start) | async-done | bytes 1048608 | tf_op jit(solution)/shard_map/all_to_all | solution.py:405
  57.3 3.4 %collective-permute-done.state_ref = bf16[2,512,128]{2,1,0:T(8,128)(2,1)} collective-permute-done((bf16[2,512,128]{2,1,0:T(8,128)(2,1)}, bf16[2,512,128]{2,1,0:T(8,128)(2,1)}, u32[]{:S(2)}, u32[]{:S(2)}) %collective-permute-start) | collective-permute-done | bytes 262176 | tf_op jit(solution)/shard_map/ppermute | solution.py:363
  60.7 0.0 copy-done.1
  60.7 6.4 %readout.1 = bf16[4,4,256,128]{3,2,1,0:T(8,128)(2,1)S(1)} custom-call(bf16[4,4,256,128]{3,2,1,0:T(8,128)(2,1)S(1)} %bitcast.24, bf16[4,4,520,128]{3,2,1,0:T(8,128)(2,1)} %bitcast.23, bf16[4,4,2,512,256]{4,3,2,1,0:T(8,128)(2,1)} %bitcast.27, f32[16,40,128]{2,1,0:T(8,128)S(1)} %chunk_factors.1.fac_ref, bf16[2,512,128]{2,1,0:T(8,128)(2,1)} %collective-permute-done.state_ref, ...), custom_call_target="tpu_custom_call" | custom-call | flops 2147483648 | bytes 10649600 | tf_op jit(solution)/shard_map/readout/pallas_call | solution.py:326
  67.1 20.2 %all_to_all.16 = bf16[16,256,128]{2,1,0:T(8,128)(2,1)S(1)} all-to-all(bf16[16,256,128]{2,1,0:T(8,128)(2,1)S(1)} %bitcast.25), channel_id=1, replica_groups=mesh['mem'=4,'hi'=2,'lo'=4] {'mem','lo'}, dimensions={0} | all-to-all | bytes 2097152 | tf_op jit(solution)/shard_map/all_to_all | solution.py:411
  87.3 1.6 %copy.8 = bf16[1,128,32,128]{3,2,1,0:T(8,128)(2,1)} copy(bf16[1,128,32,128]{3,1,2,0:T(8,128)(2,1)S(1)} %bitcast.28) | data formatting | bytes 2097152 | tf_op jit(solution)/shard_map/broadcast_in_dim | solution.py:412
Async XLA Ops:
  39.0 11.2 %copy-start = (bf16[16,520,128]{2,1,0:T(8,128)(2,1)}, bf16[16,520,128]{2,1,0:T(8,128)(2,1)S(1)}, u32[]{:S(2)}) copy-start(bf16[16,520,128]{2,1,0:T(8,128)(2,1)S(1)} %all_to_all.15.meta_ref.kv_ref) | copy-start | bytes 6389764
  39.0 18.3 %all-to-all-start = ((bf16[16,256,128]{2,1,0:T(8,128)(2,1)}), bf16[16,256,128]{2,1,0:T(8,128)(2,1)S(1)}, u32[]{:S(2)}, u32[]{:S(2)}) async-start(bf16[16,256,128]{2,1,0:T(8,128)(2,1)} %get-tuple-element.8), calls=%async_computation | async-start | bytes 2097152 | tf_op jit(solution)/shard_map/all_to_all | solution.py:405
  44.8 15.9 %collective-permute-start = (bf16[2,512,128]{2,1,0:T(8,128)(2,1)}, bf16[2,512,128]{2,1,0:T(8,128)(2,1)}, u32[]{:S(2)}, u32[]{:S(2)}) collective-permute-start(bf16[2,512,128]{2,1,0:T(8,128)(2,1)} %get-tuple-element.10), channel_id=1, source_target_pairs={{0,4},{1,5},{2,6},{3,7},{8,12},{9,13},{10,14},{11,15},{16,20},{17,... | collective-permute-start | bytes 786440 | tf_op jit(solution)/shard_map/ppermute | solution.py:363
  50.2 10.5 %copy-start.1 = (f32[4096]{0:T(1024)S(1)}, f32[4096]{0:T(1024)}, u32[]{:S(2)}) copy-start(f32[4096]{0:T(1024)} %param.13) | copy-start | bytes 49156
